TPU v7x, 256 devices: a whole 4x4x8 slice. The times are simulated.
256 devices in a mesh: lon: 16 (over y, x), lat: 8 (over z), mem: 2 (over core).
Axes of the slice: x: 4, y: 4, z: 8, core: 2. Of those that a mesh axis runs over, the one named last changes fastest.
Arguments:
- anomalies: bfloat16 [128, 128, 4096], P('mem', 'lat', 'lon'), may hold values from -6 to 6
- state_mean: float32 [128, 4096], P('lat', 'lon'), may hold values from -6 to 6
- delayed_deviation_pair: bfloat16 [2, 128, 128, 4096], P(None, 'mem', 'lat', 'lon'), may hold values from -6 to 6
- lagged_means: float32 [2, 128, 4096], P(None, 'lat', 'lon'), may hold values from -6 to 6
- courant_lon: float32 [128, 4096], P('lat', 'lon'), may hold values from -0.45 to 0.45
- courant_lat: float32 [128, 4096], P('lat', 'lon'), may hold values from -0.45 to 0.45
- ocean: int32 [128, 4096], P('lat', 'lon'), may hold values 0 or 1
- obs_values: float32 [16384, 64], P(('lon', 'lat')), may hold values from -160 to 160
- obs_variance: float32 [16384, 64], P(('lon', 'lat')), may hold values from 2048 to 32768
- obs_cells: int32 [16384, 64], P(('lon', 'lat')), may hold values from 0 to 4095
- obs_tile: int32 [16384, 1], P(('lon', 'lat')), may hold values from 0 to 127; in each aligned block of 128 rows (0 to 127, 128 to 255, ...) at most 2 rows name the same one
- obs_count: int32 [16384], P(('lon', 'lat')), may hold values from 48 to 64
Outputs:
- analysis_anomalies: bfloat16 [3, 128, 128, 4096], P(None, 'mem', 'lat', 'lon')
- analysis_mean: float32 [3, 128, 4096], P(None, 'lat', 'lon')
Inputs may be any that keep to these rules, and one draw needn't show every extreme that they name: `obs_tile`: among the 128 blocks of one tile (an aligned run of rows) no tile is named more than 2 times.
All inputs are finite; a program needn't handle non-finite values. Where the computation divides by a largest or mean magnitude, that divisor is 1e-20 or more. No bound on the sum of `ocean` on one device may be relied on, other than what follows from the above.
Results may differ from a plain program's by a relative error of at most 0.0034.
Values may be sent and summed in bfloat16 or wider, within the bound.
A program may use at most 64 MiB of HBM per device.

v0:
```python
import math

import jax
import jax.numpy as jnp
from jax import lax
from jax.sharding import Mesh
from jax.sharding import PartitionSpec as P

SUBSTEPS = 4
NS_ITERS = 8
LON = ("lon_0", "lon_1")
LON_LAT = ("lon_0", "lon_1", "lat")


def with_halo(x, sides, width, wrap):
    for axis, dim in sides:
        count, length = (lax.axis_size(axis), x.shape[dim])
        up = [(i, (i + 1) % count) for i in range(count if wrap else count - 1)]
        down = [(j, i) for i, j in up]
        last = lax.slice_in_dim(x, length - width, length, axis=dim)
        leading = lax.slice_in_dim(x, 0, width, axis=dim)
        before = lax.ppermute(last, axis, up)
        after = lax.ppermute(leading, axis, down)
        x = jnp.concatenate([before, x, after], axis=dim)
    return x


def sent_together(arrays, axis, split_dim, concat_dim, along):
    widths = [a.shape[along] for a in arrays]
    both = jnp.concatenate(arrays, axis=along)
    out = lax.all_to_all(both, axis, split_axis=split_dim, concat_axis=concat_dim, tiled=True)
    return tuple(jnp.split(out, [sum(widths[:k]) for k in range(1, len(widths))], axis=along))


def over_axes(x, axes):
    for axis in axes:
        x = lax.psum(x, axis)
    return x


def side_by_side(arrays, axis, dim, along):
    widths = [math.prod(a.shape[along:]) for a in arrays]
    both = jnp.concatenate(
        [a.reshape(*a.shape[:along], w) for a, w in zip(arrays, widths)], axis=along
    )
    out = lax.all_gather(both, axis, axis=dim, tiled=True)
    blocks = jnp.split(out, [sum(widths[:k]) for k in range(1, len(widths))], axis=along)
    return tuple((b.reshape(*out.shape[:along], *a.shape[along:]) for a, b in zip(arrays, blocks)))


def upwind(center, western, eastern, southern, northern, courant_x, courant_y, wet_mask):
    tendency = (
        jnp.maximum(courant_x, 0.0) * (center - western)
        + jnp.minimum(courant_x, 0.0) * (eastern - center)
        + jnp.maximum(courant_y, 0.0) * (center - southern)
        + jnp.minimum(courant_y, 0.0) * (northern - center)
    )
    return center - wet_mask * tendency


def inverse_root(gram, projection):
    members = gram.shape[0]
    identity = jnp.eye(members, dtype=jnp.float32)
    system = (members - 1.0) * identity + 0.5 * (gram + gram.T)
    bound = jnp.max(jnp.sum(jnp.abs(system), axis=1))
    iterate = system / bound
    accum = identity
    for sweep in range(NS_ITERS):
        factor = 1.5 * identity - 0.5 * jnp.dot(accum, iterate, precision=lax.Precision.HIGHEST)
        iterate = jnp.dot(iterate, factor, precision=lax.Precision.HIGHEST)
        accum = jnp.dot(factor, accum, precision=lax.Precision.HIGHEST)
    root = accum / jnp.sqrt(bound)
    weights = jnp.dot(
        root,
        jnp.dot(root, projection, precision=lax.Precision.HIGHEST),
        precision=lax.Precision.HIGHEST,
    )
    transform = jnp.sqrt(members - 1.0) * root
    return (transform.astype(jnp.bfloat16), weights.astype(jnp.bfloat16))


def body(
    anomalies,
    state_mean,
    delayed_deviation_pair,
    lagged_means,
    courant_lon,
    courant_lat,
    ocean,
    obs_values,
    obs_variance,
    obs_cells,
    obs_tile,
    obs_count,
):
    locally_held_samples = anomalies.shape[0]
    wet_mask = ocean.astype(jnp.float32)
    coefficients = jnp.stack([courant_lon, courant_lat, wet_mask])
    sample_surfaces = jnp.concatenate([anomalies.astype(jnp.float32), state_mean[None]], 0)
    stacked = jnp.concatenate([sample_surfaces, coefficients], 0)
    widened = with_halo(stacked, ((LON, 2),), SUBSTEPS, True)
    extended = with_halo(widened.astype(jnp.bfloat16), (("lat", 1),), SUBSTEPS, False).astype(
        widened.dtype
    )
    field_count = sample_surfaces.shape[0]
    sample_surfaces = extended[:field_count]
    beside_all = extended[field_count:]
    for substep in range(SUBSTEPS):
        inner = beside_all[
            :,
            substep + 1 : beside_all.shape[1] - substep - 1,
            substep + 1 : beside_all.shape[2] - substep - 1,
        ]
        sample_surfaces = upwind(
            sample_surfaces[:, 1:-1, 1:-1],
            sample_surfaces[:, 1:-1, :-2],
            sample_surfaces[:, 1:-1, 2:],
            sample_surfaces[:, :-2, 1:-1],
            sample_surfaces[:, 2:, 1:-1],
            inner[0],
            inner[1],
            inner[2],
        )
    predicted_sample_vectors = sample_surfaces[:locally_held_samples].astype(jnp.bfloat16)
    prior_mean = sample_surfaces[locally_held_samples]
    total_cells = prior_mean.shape[0] * prior_mean.shape[1]
    cell_table = predicted_sample_vectors.reshape(locally_held_samples, total_cells).T
    tiles = lax.axis_size(LON_LAT)
    block_total = obs_values.shape[0]
    slot_width = obs_values.shape[1]
    capacity = 2 * block_total // tiles
    target = obs_tile[:, 0]
    block_order = jnp.arange(block_total, dtype=jnp.int32)
    same_target = target[:, None] == target[None, :]
    earlier = block_order[:, None] > block_order[None, :]
    position = jnp.sum((same_target & earlier).astype(jnp.int32), 1)
    destination = target * capacity + position
    placement_table = (
        destination[:, None] == jnp.arange(tiles * capacity, dtype=jnp.int32)[None, :]
    ).astype(jnp.float32)
    valid = jnp.arange(slot_width, dtype=jnp.int32)[None, :] < obs_count[:, None]
    weight = jnp.where(valid, 1.0 / obs_variance, 0.0)
    packed = jnp.concatenate([obs_values, weight, obs_cells.astype(jnp.float32)], 1)
    placed = lax.dot_general(
        placement_table, packed, (((0,), (0,)), ((), ())), precision=lax.Precision.HIGHEST
    ).reshape(tiles, capacity, 3, slot_width)
    arrived_values = sent_together(
        (placed[:, :, 0], placed[:, :, 1], placed[:, :, 2]), LON_LAT, 0, 0, 1
    )
    grid_cells = arrived_values[2].reshape(-1).astype(jnp.int32)
    obs_weight = arrived_values[1].reshape(-1)
    obs_misfit = (arrived_values[0].reshape(-1) - prior_mean.reshape(-1)[grid_cells]).astype(
        jnp.bfloat16
    )
    observed = jnp.take(cell_table, grid_cells, axis=0)
    weighted = (observed.astype(jnp.float32) * obs_weight[:, None]).astype(jnp.bfloat16)
    observed_all = lax.all_gather(observed, "mem", axis=1, tiled=True)
    gram_part = lax.dot_general(
        weighted, observed_all, (((0,), (0,)), ((), ())), preferred_element_type=jnp.float32
    )
    projection_part = lax.dot_general(
        weighted, obs_misfit, (((0,), (0,)), ((), ())), preferred_element_type=jnp.float32
    )
    gram_part, projection_part = (
        over_axes(gram_part, LON_LAT),
        over_axes(projection_part, LON_LAT),
    )
    gram, projection = side_by_side((gram_part, projection_part), "mem", 0, 1)
    transform, weights = inverse_root(gram, projection)
    marine_sample_vectors = jnp.concatenate(
        [predicted_sample_vectors[None], delayed_deviation_pair], 0
    )
    flat_states = marine_sample_vectors.reshape(3, locally_held_samples, total_cells)
    first_member = lax.axis_index("mem") * locally_held_samples
    own_columns = lax.dynamic_slice_in_dim(transform, first_member, locally_held_samples, 1)
    segment = lax.all_gather(marine_sample_vectors, "mem", axis=1, tiled=True)
    length = segment.shape[1]
    flat_segment = segment.reshape(3, length, total_cells)
    moved_sum = jnp.einsum(
        "nk,snc->skc", own_columns, flat_segment, preferred_element_type=jnp.float32
    )
    increment_sum = jnp.einsum(
        "n,snc->sc", weights, flat_segment, preferred_element_type=jnp.float32
    )
    wet_flat = wet_mask.reshape(-1)
    states_float = flat_states.astype(jnp.float32)
    blended = (states_float + wet_flat * (moved_sum - states_float)).astype(jnp.bfloat16)
    analysis_anomalies = blended.reshape(marine_sample_vectors.shape)
    state_means = jnp.concatenate([prior_mean[None], lagged_means], 0)
    analysis_mean = state_means + wet_mask * increment_sum.reshape(state_means.shape)
    return (analysis_anomalies, analysis_mean)


def solution(mesh):
    finer = Mesh(
        mesh.devices.reshape(4, 4, mesh.shape["lat"], mesh.shape["mem"]),
        ("lon_0", "lon_1", "lat", "mem"),
    )
    return jax.shard_map(
        body,
        mesh=finer,
        in_specs=(
            P("mem", "lat", LON),
            P("lat", LON),
            P(None, "mem", "lat", LON),
            P(None, "lat", LON),
            P("lat", LON),
            P("lat", LON),
            P("lat", LON),
            P(LON_LAT, None),
            P(LON_LAT, None),
            P(LON_LAT, None),
            P(LON_LAT, None),
            P(LON_LAT),
        ),
        out_specs=(P(None, "mem", "lat", LON), P(None, "lat", LON)),
        check_vma=False,
    )
```

profile of v0, /device:TPU:1, one launch (start us, length us, event | category | flops | bytes accessed | tf_op | source)
XLA Modules:
  0.0 339.2 jit_solution(2044609461510425592)
XLA Ops:
  7.2 1.1 convert_dynamic-update-slice_fusion
  11.7 2.1 collective-permute-start
  14.1 3.8 %collective-permute-start.1 = (bf16[68,16,4]{0,1,2:T(8,128)(2,1)S(1)}, bf16[68,16,4]{0,1,2:T(8,128)(2,1)S(1)}, u32[]{:S(2)}, u32[]{:S(2)}) collective-permute-start(bf16[68,16,4]{0,1,2:T(8,128)(2,1)S(1)} %copy.74), channel_id=1, source_target_pairs={{16,0},{32,16},{48,32},{64,48},{80,64},{96,80},{112,96},{128,112},... | collective-permute-start | bytes 26120 | tf_op jit(solution)/shard_map/ppermute | solution.py:23
  20.0 3.6 %collective-permute-start.2 = (bf16[68,4,264]{2,1,0:T(4,128)(2,1)S(1)}, bf16[68,4,264]{2,1,0:T(4,128)(2,1)S(1)}, u32[]{:S(2)}, u32[]{:S(2)}) collective-permute-start(bf16[68,4,264]{2,1,0:T(4,128)(2,1)S(1)} %get-tuple-element.32), channel_id=1, source_target_pairs={{0,2},{2,4},{4,6},{6,8},{8,10},{10,12},{12,14},{1,3},{3,5},{5,7},{... | collective-permute-start | bytes 430856 | tf_op jit(solution)/shard_map/ppermute | solution.py:22
  23.6 1.3 collective-permute-start.3
  25.4 0.9 reshape.99
  26.3 16.5 %all-to-all-start = ((f32[128,1,384]{2,1,0:T(1,128)}), f32[128,1,384]{2,1,0:T(1,128)S(1)}, u32[]{:S(2)}, u32[]{:S(2)}) async-start(f32[128,1,384]{2,1,0:T(1,128)} %reshape.99), calls=%async_computation | async-start | bytes 393216 | tf_op jit(solution)/shard_map/all_to_all | solution.py:31
  43.7 1.3 maximum_convert_fusion
  44.9 2.6 fusion.28
  47.6 2.6 fusion.19
  50.3 2.6 fusion.10
  53.0 1.2 fusion.50
  55.0 2.5 pad_maximum_fusion
  58.3 1.1 reduce.2
  60.1 57.8 %gather_fusion = bf16[16384,64]{1,0:T(8,128)(2,1)} fusion(bf16[4096,64]{1,0:T(8,128)(2,1)S(1)} %bitcast.187, s32[16384]{0:T(1024)S(1)} %broadcast_clamp_fusion), kind=kCustom, calls=%fused_computation | custom fusion | bytes 4259840 | tf_op jit(solution)/shard_map/jit(_take)/gather | solution.py:155
  118.0 11.6 %broadcast_select_fusion = bf16[16384,64]{1,0:T(8,128)(2,1)} fusion(bf16[16384,64]{1,0:T(8,128)(2,1)} %gather_fusion, pred[16384]{0:T(1024)(128)(4,1)S(1)} %compare_and_fusion), kind=kLoop, calls=%fused_computation.8 | loop fusion | flops 1048576 | bytes 4210688 | tf_op jit(solution)/shard_map/jit(_take)/select_n | solution.py:155
  129.5 4.9 %copy.81 = bf16[16384,64]{0,1:T(8,128)(2,1)} copy(bf16[16384,64]{1,0:T(8,128)(2,1)} %broadcast_select_fusion) | data formatting | bytes 4194304 | tf_op jit(solution)/shard_map/jit(_take)/select_n | solution.py:155
  134.5 1.2 copy-done
  135.7 1.3 concatenate.36
  138.2 1.0 concatenate.35
  139.9 90.5 %gather_fusion.1 = f32[16384]{0:T(1024)S(1)} fusion(f32[4096]{0:T(1024)S(1)} %bitcast.186, s32[16384]{0:T(1024)S(1)} %broadcast_clamp_fusion), kind=kCustom, calls=%fused_computation.1 | custom fusion | bytes 196608 | tf_op jit(solution)/shard_map/gather | solution.py:152
  230.7 4.7 %fusion.44 = f32[64]{0:T(128)S(1)} fusion(bf16[16384,1]{0,1:T(2,128)(2,1)S(1)} %reshape.88, bf16[16384,64]{1,0:T(8,128)(2,1)} %broadcast_select_fusion, f32[16384]{0:T(1024)S(1)} %mul.368), kind=kOutput, calls=%fused_computation.72 | convolution fusion | flops 5242880 | bytes 2195712 | tf_op jit(solution)/shard_map/dot_general | solution.py:161
  235.4 4.2 %reshape.65 = bf16[3,128,4096]{2,1,0:T(8,128)(2,1)S(1)} reshape(bf16[3,128,16,256]{3,2,1,0:T(8,128)(2,1)} %all-gather.3.cloned.1.call-done) | data formatting | bytes 6291456 | tf_op jit(solution)/shard_map/reshape | solution.py:178
  239.6 9.7 %fusion.35 = f32[64,128]{1,0:T(8,128)S(1)} fusion(bf16[16384,128]{0,1:T(8,128)(2,1)} %all-gather.5.cloned.1.call-done, bf16[16384,64]{1,0:T(8,128)(2,1)} %broadcast_select_fusion, f32[16384]{0:T(1024)S(1)} %mul.368), kind=kOutput, calls=%fused_computation.52 | convolution fusion | flops 271581184 | bytes 6389760 | tf_op jit(solution)/shard_map/dot_general | solution.py:158
  249.4 13.4 %all-reduce.2 = (f32[64]{0:T(128)S(1)}, f32[64,128]{1,0:T(8,128)S(1)}) all-reduce(f32[64]{0:T(128)S(1)} %fusion.44, f32[64,128]{1,0:T(8,128)S(1)} %fusion.35), channel_id=1, replica_groups=mesh['lon_0'=4,'lon_1'=4,'lat'=8,'mem'=2] {'lon_0'}, use_global_device_ids=true, to_apply=%region_4.5 | all-reduce | flops 8256 | bytes 66048 | tf_op jit(solution)/shard_map/psum | solution.py:37
  262.8 13.7 %all-reduce.1 = (f32[64]{0:T(128)S(1)}, f32[64,128]{1,0:T(8,128)S(1)}) all-reduce(f32[64]{0:T(128)S(1)} %get-tuple-element.6, f32[64,128]{1,0:T(8,128)S(1)} %get-tuple-element.7), channel_id=1, replica_groups=mesh['lon_0'=4,'lon_1'=4,'lat'=8,'mem'=2] {'lon_1'}, use_global_device_ids=true, to_apply=%region_5.6 | all-reduce | flops 8256 | bytes 66048 | tf_op jit(solution)/shard_map/psum | solution.py:37
  276.5 23.1 %all-reduce = (f32[64,1]{1,0:T(8,128)S(1)}, f32[64,128]{1,0:T(8,128)S(1)}) all-reduce(f32[64,1]{1,0:T(8,128)S(1)} %copy.82, f32[64,128]{1,0:T(8,128)S(1)} %get-tuple-element.5), channel_id=1, replica_groups=mesh['lon_0'=4,'lon_1'=4,'lat'=8,'mem'=2] {'lat'}, use_global_device_ids=true, to_apply=%region_6.7 | all-reduce | flops 8256 | bytes 66048 | tf_op jit(solution)/shard_map/psum | solution.py:37
  299.6 19.4 %all_gather.11 = f32[128,129]{1,0:T(8,128)S(1)} all-gather(f32[64,129]{1,0:T(8,128)S(1)} %pad_maximum_fusion.5), channel_id=1, replica_groups=mesh['lon_0'=4,'lon_1'=4,'lat'=8,'mem'=2] {'mem'}, dimensions={0}, use_global_device_ids=true | all-gather | bytes 99072 | tf_op jit(solution)/shard_map/all_gather | solution.py:46
  319.9 0.8 fusion.43
  320.7 0.9 fusion.82
  327.2 2.3 fusion.3
  329.6 1.6 copy.93
  (113 shorter events, 18.5 us)
Async XLA Ops:
  7.2 10.7 %copy-start.5 = (s32[128,64]{0,1:T(8,128)S(1)}, s32[128,64]{0,1:T(8,128)}, u32[]{:S(2)}) copy-start(s32[128,64]{0,1:T(8,128)} %param.21) | copy-start | bytes 98308
  7.2 10.7 %copy-start.10 = (s32[128,1]{0,1:T(1,128)S(1)}, s32[128,1]{0,1:T(1,128)}, u32[]{:S(2)}) copy-start(s32[128,1]{0,1:T(1,128)} %param.22) | copy-start | bytes 1540
  7.2 10.9 %copy-start.6 = (f32[128,64]{0,1:T(8,128)S(1)}, f32[128,64]{0,1:T(8,128)}, u32[]{:S(2)}) copy-start(f32[128,64]{0,1:T(8,128)} %param.20) | copy-start | bytes 98308
  7.2 10.9 %copy-start.9 = (s32[128]{0:T(128)S(1)}, s32[128]{0:T(128)}, u32[]{:S(2)}) copy-start(s32[128]{0:T(128)} %param.23) | copy-start | bytes 1540
  7.2 10.9 %copy-start.7 = (f32[128,64]{0,1:T(8,128)S(1)}, f32[128,64]{0,1:T(8,128)}, u32[]{:S(2)}) copy-start(f32[128,64]{0,1:T(8,128)} %param.19) | copy-start | bytes 98308
  11.7 7.1 %collective-permute-start = (bf16[68,16,4]{0,1,2:T(8,128)(2,1)S(1)}, bf16[68,16,4]{0,1,2:T(8,128)(2,1)S(1)}, u32[]{:S(2)}, u32[]{:S(2)}) collective-permute-start(bf16[68,16,4]{0,1,2:T(8,128)(2,1)S(1)} %copy.73), channel_id=1, source_target_pairs={{0,16},{16,32},{32,48},{48,64},{64,80},{80,96},{96,112},{112,128},... | collective-permute-start | bytes 26120 | tf_op jit(solution)/shard_map/ppermute | solution.py:22
  14.1 5.0 %collective-permute-start.1 = (bf16[68,16,4]{0,1,2:T(8,128)(2,1)S(1)}, bf16[68,16,4]{0,1,2:T(8,128)(2,1)S(1)}, u32[]{:S(2)}, u32[]{:S(2)}) collective-permute-start(bf16[68,16,4]{0,1,2:T(8,128)(2,1)S(1)} %copy.74), channel_id=1, source_target_pairs={{16,0},{32,16},{48,32},{64,48},{80,64},{96,80},{112,96},{128,112},... | collective-permute-start | bytes 26120 | tf_op jit(solution)/shard_map/ppermute | solution.py:23
  20.0 23.1 %collective-permute-start.2 = (bf16[68,4,264]{2,1,0:T(4,128)(2,1)S(1)}, bf16[68,4,264]{2,1,0:T(4,128)(2,1)S(1)}, u32[]{:S(2)}, u32[]{:S(2)}) collective-permute-start(bf16[68,4,264]{2,1,0:T(4,128)(2,1)S(1)} %get-tuple-element.32), channel_id=1, source_target_pairs={{0,2},{2,4},{4,6},{6,8},{8,10},{10,12},{12,14},{1,3},{3,5},{5,7},{... | collective-permute-start | bytes 430856 | tf_op jit(solution)/shard_map/ppermute | solution.py:22
  23.6 19.5 %collective-permute-start.3 = (bf16[68,4,264]{2,1,0:T(4,128)(2,1)S(1)}, bf16[68,4,264]{2,1,0:T(4,128)(2,1)S(1)}, u32[]{:S(2)}, u32[]{:S(2)}) collective-permute-start(bf16[68,4,264]{2,1,0:T(4,128)(2,1)S(1)} %get-tuple-element.33), channel_id=1, source_target_pairs={{2,0},{4,2},{6,4},{8,6},{10,8},{12,10},{14,12},{3,1},{5,3},{7,5},{... | collective-permute-start | bytes 430856 | tf_op jit(solution)/shard_map/ppermute | solution.py:23
  26.3 31.5 %all-to-all-start = ((f32[128,1,384]{2,1,0:T(1,128)}), f32[128,1,384]{2,1,0:T(1,128)S(1)}, u32[]{:S(2)}, u32[]{:S(2)}) async-start(f32[128,1,384]{2,1,0:T(1,128)} %reshape.99), calls=%async_computation | async-start | bytes 393216 | tf_op jit(solution)/shard_map/all_to_all | solution.py:31
  42.8 192.5 %all-gather.3.cloned.1.call-start = ((), (), s32[]{:S(2)}) async-start(), calls=%async_computation.1 | async-start | bytes 4718592 | tf_op jit(solution)/shard_map/all_gather | solution.py:176
  57.5 182.1 %all-gather.5.cloned.1.call-start = ((), (), s32[]{:S(2)}) async-start(), calls=%async_computation.2 | async-start | bytes 6291456 | tf_op jit(solution)/shard_map/all_gather | solution.py:157
  134.4 1.2 copy-start
  134.4 2.5 copy-start.3
  320.7 6.5 %copy-start.8 = (f32[2,2,8,128]{3,1,2,0:T(2,128)S(1)}, f32[2,2,8,128]{3,1,2,0:T(2,128)}, u32[]{:S(2)}) copy-start(f32[2,2,8,128]{3,1,2,0:T(2,128)} %copy.91) | copy-start | bytes 49156
  329.6 2.1 copy-start.1
  329.6 2.1 copy-start.2
  329.6 2.1 copy-start.4
Sparse Core Ops, SparseCore 0:
  57.6 21.3 all-gather.2
  134.6 22.8 all-gather.4
where the time goes:
time: 340 us; the launch traced here: 339 us
  local copies, waits for them, and re-layouts  171 us (50%)
  blocking collectives  69.6 us (20%)
  other arithmetic  31.2 us (9%)
  starting transfers between devices  27.7 us (8%)
  matrix products  24 us (7%)
  between operations  15.4 us (5%)
    gather x1, local copies, waits for them, and re-layouts, body(): prior_mean.reshape(-1)[grid_cells]  90.5 us
    gather x1, local copies, waits for them, and re-layouts, body(): observed = jnp.take(cell_table, grid_cells, axis=0)  57.8 us
    psum x3, blocking collectives, over_axes(): x = lax.psum(x, axis)  50.1 us
    all_gather x1, blocking collectives, side_by_side(): out = lax.all_gather(both, axis, axis=dim, tiled=True)  19.4 us
    all_to_all x1, starting transfers between devices, sent_together(): lax.all_to_all(both, axis, split_axis=split_dim, concat_axis=concat_dim,...  16.5 us
    select_n x2, other arithmetic, body(): observed = jnp.take(cell_table, grid_cells, axis=0)  11.6 us
    dot_general x1, matrix products, body(): lax.dot_general(weighted, observed_all, (((0,), (0,)), ((), ())), preferr...  9.73 us
    sub x4, other arithmetic, upwind(): return center - wet_mask * tendency  8.93 us
  transfers between devices with their start and end apart: 7, of which 0 were waited for; matrix products, arithmetic and copies ran while one was open for 58% of the time, Pallas kernels for 0%

commit v1 on v0

--- a/solution.py
+++ b/solution.py
@@ -124,7 +124,6 @@
     predicted_sample_vectors = sample_surfaces[:locally_held_samples].astype(jnp.bfloat16)
     prior_mean = sample_surfaces[locally_held_samples]
     total_cells = prior_mean.shape[0] * prior_mean.shape[1]
-    cell_table = predicted_sample_vectors.reshape(locally_held_samples, total_cells).T
     tiles = lax.axis_size(LON_LAT)
     block_total = obs_values.shape[0]
     slot_width = obs_values.shape[1]
@@ -149,17 +148,36 @@
     )
     grid_cells = arrived_values[2].reshape(-1).astype(jnp.int32)
     obs_weight = arrived_values[1].reshape(-1)
-    obs_misfit = (arrived_values[0].reshape(-1) - prior_mean.reshape(-1)[grid_cells]).astype(
-        jnp.bfloat16
-    )
-    observed = jnp.take(cell_table, grid_cells, axis=0)
-    weighted = (observed.astype(jnp.float32) * obs_weight[:, None]).astype(jnp.bfloat16)
-    observed_all = lax.all_gather(observed, "mem", axis=1, tiled=True)
+    scaled_value = obs_weight * arrived_values[0].reshape(-1)
+    rows, columns = (prior_mean.shape[0], prior_mean.shape[1])
+    planes = []
+    for plane in (obs_weight, scaled_value):
+        upper = plane.astype(jnp.bfloat16)
+        planes += [upper, (plane - upper.astype(jnp.float32)).astype(jnp.bfloat16)]
+    in_row = (grid_cells // columns)[None, :] == jnp.arange(rows, dtype=jnp.int32)[:, None]
+    in_column = (grid_cells % columns)[None, :] == jnp.arange(columns, dtype=jnp.int32)[:, None]
+    spread = jnp.concatenate(
+        [jnp.where(in_row, p[None, :], jnp.zeros((), jnp.bfloat16)) for p in planes], 0
+    )
+    sums = lax.dot_general(
+        spread,
+        in_column.astype(jnp.bfloat16),
+        (((1,), (1,)), ((), ())),
+        preferred_element_type=jnp.float32,
+    ).reshape(2, 2, rows, columns)
+    cell_weight = sums[0, 0] + sums[0, 1]
+    cell_misfit = (sums[1, 0] + sums[1, 1]) - cell_weight * prior_mean
+    observed = predicted_sample_vectors.reshape(locally_held_samples, total_cells)
+    weighted = (observed.astype(jnp.float32) * cell_weight.reshape(-1)).astype(jnp.bfloat16)
+    observed_all = lax.all_gather(observed, "mem", axis=0, tiled=True)
     gram_part = lax.dot_general(
-        weighted, observed_all, (((0,), (0,)), ((), ())), preferred_element_type=jnp.float32
+        weighted, observed_all, (((1,), (1,)), ((), ())), preferred_element_type=jnp.float32
     )
     projection_part = lax.dot_general(
-        weighted, obs_misfit, (((0,), (0,)), ((), ())), preferred_element_type=jnp.float32
+        observed,
+        cell_misfit.reshape(-1).astype(jnp.bfloat16),
+        (((1,), (0,)), ((), ())),
+        preferred_element_type=jnp.float32,
     )
     gram_part, projection_part = (
         over_axes(gram_part, LON_LAT),

time: 340 us -> 170 us (0.50)
  local copies, waits for them, and re-layouts: 171 us -> 15.7 us
  waiting for transfers between devices: 0.07 us -> 13.7 us
  other arithmetic: 31.2 us -> 18.3 us
  matrix products: 24 us -> 14.5 us
  blocking collectives: 69.6 us -> 65.6 us
    gather x2 -> x0, local copies, waits for them, and re-layouts: 148 us -> none  [the longest x1 90.5 us: body(): prior_mean.reshape(-1)[grid_cells]]
    select_n x2, other arithmetic: 11.6 us -> 0.4 us  [the longest x1 0.34 us: body(): jnp.where(in_row, p[None, :], jnp.zeros((), jnp.bfloat16))]
    dot_general x2 -> x3, matrix products: 14.4 us -> 4.92 us  [the longest x1 2.97 us: body(): lax.dot_general(spread, in_column.astype(jnp.bfloat16), (((1,), (1,)), ((...]
    all_to_all x1, waiting for transfers between devices: 0.01 us -> 7.95 us  [sent_together(): lax.all_to_all(both, axis, split_axis=split_dim, concat_axis=concat_dim,...]
    psum x3, blocking collectives: 50.1 us -> 44.5 us  [over_axes(): x = lax.psum(x, axis)]
    select_n x1 -> x0, local copies, waits for them, and re-layouts: 4.91 us -> none  [body(): observed = jnp.take(cell_table, grid_cells, axis=0)]
    ppermute x2, waiting for transfers between devices: 0.01 us -> 4.01 us  [with_halo(): after = lax.ppermute(leading, axis, down)]
  transfers between devices with their start and end apart: 7 -> 7, of which waited for: 0 -> 4; matrix products, arithmetic and copies ran while one was open for 58% -> 13% of each run, Pallas kernels for 0% -> 0%
where the time goes in v1:
time: 170 us; the launch traced here: 169 us
  blocking collectives  65.6 us (39%)
  starting transfers between devices  25.7 us (15%)
  other arithmetic  18.3 us (11%)
  local copies, waits for them, and re-layouts  15.7 us (9%)
  between operations  15.4 us (9%)
  matrix products  14.5 us (9%)
  waiting for transfers between devices  13.7 us (8%)
    psum x3, blocking collectives, over_axes(): x = lax.psum(x, axis)  44.5 us
    all_gather x1, blocking collectives, side_by_side(): out = lax.all_gather(both, axis, axis=dim, tiled=True)  21.1 us
    all_to_all x1, starting transfers between devices, sent_together(): lax.all_to_all(both, axis, split_axis=split_dim, concat_axis=concat_dim,...  14.7 us
    sub x4, other arithmetic, upwind(): return center - wet_mask * tendency  8.92 us
    all_to_all x1, waiting for transfers between devices, sent_together(): lax.all_to_all(both, axis, split_axis=split_dim, concat_axis=concat_dim,...  7.95 us
    unnamed x30, local copies, waits for them, and re-layouts  5.93 us
    ppermute x2, starting transfers between devices, with_halo(): before = lax.ppermute(last, axis, up)  5.65 us
    ppermute x2, starting transfers between devices, with_halo(): after = lax.ppermute(leading, axis, down)  5.26 us
  transfers between devices with their start and end apart: 7, of which 4 were waited for; matrix products, arithmetic and copies ran while one was open for 13% of the time, Pallas kernels for 0%

profile of v1, /device:TPU:1, one launch (start us, length us, event | category | flops | bytes accessed | tf_op | source)
XLA Modules:
  0.0 169.0 jit_solution(13560718712493647950)
XLA Ops:
  7.2 1.1 convert_dynamic-update-slice_fusion
  8.3 0.7 bitcast_dynamic-update-slice_fusion.3
  11.7 2.1 %collective-permute-start = (bf16[68,16,4]{0,1,2:T(8,128)(2,1)S(1)}, bf16[68,16,4]{0,1,2:T(8,128)(2,1)S(1)}, u32[]{:S(2)}, u32[]{:S(2)}) collective-permute-start(bf16[68,16,4]{0,1,2:T(8,128)(2,1)S(1)} %copy.67), channel_id=1, source_target_pairs={{0,16},{16,32},{32,48},{48,64},{64,80},{80,96},{96,112},{112,128},... | collective-permute-start | bytes 26120 | tf_op jit(solution)/shard_map/ppermute | solution.py:22
  14.1 3.8 %collective-permute-start.1 = (bf16[68,16,4]{0,1,2:T(8,128)(2,1)S(1)}, bf16[68,16,4]{0,1,2:T(8,128)(2,1)S(1)}, u32[]{:S(2)}, u32[]{:S(2)}) collective-permute-start(bf16[68,16,4]{0,1,2:T(8,128)(2,1)S(1)} %copy.68), channel_id=1, source_target_pairs={{16,0},{32,16},{48,32},{64,48},{80,64},{96,80},{112,96},{128,112},... | collective-permute-start | bytes 26120 | tf_op jit(solution)/shard_map/ppermute | solution.py:23
  19.9 3.6 %collective-permute-start.2 = (bf16[68,4,264]{2,1,0:T(4,128)(2,1)S(1)}, bf16[68,4,264]{2,1,0:T(4,128)(2,1)S(1)}, u32[]{:S(2)}, u32[]{:S(2)}) collective-permute-start(bf16[68,4,264]{2,1,0:T(4,128)(2,1)S(1)} %get-tuple-element.34), channel_id=1, source_target_pairs={{0,2},{2,4},{4,6},{6,8},{8,10},{10,12},{12,14},{1,3},{3,5},{5,7},{... | collective-permute-start | bytes 430856 | tf_op jit(solution)/shard_map/ppermute | solution.py:22
  23.5 1.5 collective-permute-start.3
  24.9 1.2 collective-permute-done.2
  26.2 4.0 %collective-permute-done.3 = bf16[68,4,264]{2,1,0:T(4,128)(2,1)S(1)} collective-permute-done((bf16[68,4,264]{2,1,0:T(4,128)(2,1)S(1)}, bf16[68,4,264]{2,1,0:T(4,128)(2,1)S(1)}, u32[]{:S(2)}, u32[]{:S(2)}) %collective-permute-start.3) | collective-permute-done | bytes 143648 | tf_op jit(solution)/shard_map/ppermute | solution.py:23
  30.7 1.3 maximum_convert_fusion
  32.0 2.6 %fusion.30 = f32[65,22,262]{2,1,0:T(8,128)S(1)} fusion(f32[68,24,264]{2,1,0:T(8,128)S(1)} %maximum_convert_fusion, f32[22,262]{1,0:T(8,128)S(1)} %get-tuple-element.59, f32[22,262]{1,0:T(8,128)S(1)} %get-tuple-element.32, f32[22,262]{1,0:T(8,128)S(1)} %get-tuple-element.58, f32[22,262]{1,0:T(8,128)S(1)} %get-tuple-element.22, ...), kind=kLoop, calls=%fused_computation.41 | loop fusion | flops 4870580 | bytes 9107120 | tf_op jit(solution)/shard_map/sub | solution.py:58
  34.7 2.6 %fusion.21 = f32[65,20,260]{2,1,0:T(8,128)S(1)} fusion(f32[65,22,262]{2,1,0:T(8,128)S(1)} %fusion.30, f32[20,260]{1,0:T(8,128)S(1)} %get-tuple-element.61, f32[20,260]{1,0:T(8,128)S(1)} %get-tuple-element.30, f32[20,260]{1,0:T(8,128)S(1)} %get-tuple-element.60, f32[20,260]{1,0:T(8,128)S(1)} %get-tuple-element.18, f32[20,260]{1,0:T(8,128)S(1)} %convert_bitcast_fusion.1), kind=kLoop, calls=%fused_computation.28 | loop fusion | flops 4394000 | bytes 8216000 | tf_op jit(solution)/shard_map/sub | solution.py:58
  37.4 2.6 %fusion.12 = f32[65,18,258]{2,1,0:T(8,128)S(1)} fusion(f32[65,20,260]{2,1,0:T(8,128)S(1)} %fusion.21, f32[18,258]{1,0:T(8,128)S(1)} %get-tuple-element.63, f32[18,258]{1,0:T(8,128)S(1)} %get-tuple-element.28, f32[18,258]{1,0:T(8,128)S(1)} %get-tuple-element.62, f32[18,258]{1,0:T(8,128)S(1)} %get-tuple-element.14, f32[18,258]{1,0:T(8,128)S(1)} %convert_bitcast_fusion), kind=kLoop, calls=%fused_computation.15 | loop fusion | flops 3924180 | bytes 7337520 | tf_op jit(solution)/shard_map/sub | solution.py:58
  40.1 1.2 fusion.56
  41.3 1.0 copy.84
  43.8 0.9 reshape.150
  44.7 14.7 %all-to-all-start = ((f32[128,1,384]{2,1,0:T(1,128)}), f32[128,1,384]{2,1,0:T(1,128)S(1)}, u32[]{:S(2)}, u32[]{:S(2)}) async-start(f32[128,1,384]{2,1,0:T(1,128)} %reshape.150), calls=%async_computation | async-start | bytes 393216 | tf_op jit(solution)/shard_map/all_to_all | solution.py:31
  59.5 1.3 concatenate.39
  60.8 1.0 concatenate.38
  61.9 1.3 pad_maximum_fusion
  63.2 8.0 %all-to-all-done = f32[128,1,384]{2,1,0:T(1,128)S(1)} async-done(((f32[128,1,384]{2,1,0:T(1,128)}), f32[128,1,384]{2,1,0:T(1,128)S(1)}, u32[]{:S(2)}, u32[]{:S(2)}) %all-to-all-start) | async-done | bytes 196640 | tf_op jit(solution)/shard_map/all_to_all | solution.py:31
  71.7 1.1 reduce.2
  73.9 3.0 %fusion = f32[64,256]{1,0:T(8,128)S(1)} fusion(s32[16384]{0:T(1024)S(1)} %get-tuple-element.55, bf16[16,16384]{1,0:T(8,128)(2,1)S(1)} %get-tuple-element.49, bf16[16,16384]{1,0:T(8,128)(2,1)S(1)} %get-tuple-element.50, bf16[16,16384]{1,0:T(8,128)(2,1)S(1)} %get-tuple-element.51, bf16[16,16384]{1,0:T(8,128)(2,1)S(1)} %get-tuple-element.48), kind=kOutput, calls=%fused_computation.1 | convolution fusion | flops 549453824 | bytes 2228224 | tf_op jit(solution)/shard_map/dot_general | solution.py:162
  77.2 1.7 %fusion.66 = f32[64,128]{1,0:T(8,128)S(1)} fusion(bf16[128,4096]{1,0:T(8,128)(2,1)} %all-gather.5.cloned.1.call-done, bf16[64,4096]{1,0:T(8,128)(2,1)S(1)} %bitcast.200, f32[4096]{0:T(1024)S(1)} %bitcast.207), kind=kOutput, calls=%fused_computation.102 | convolution fusion | flops 67895296 | bytes 1622016 | tf_op jit(solution)/shard_map/dot_general | solution.py:173
  78.9 11.4 %all-reduce.2 = (f32[64]{0:T(128)S(1)}, f32[64,128]{1,0:T(8,128)S(1)}) all-reduce(f32[64]{0:T(128)S(1)} %convolution_bitcast_fusion.3, f32[64,128]{1,0:T(8,128)S(1)} %fusion.66), channel_id=1, replica_groups=mesh['lon_0'=4,'lon_1'=4,'lat'=8,'mem'=2] {'lon_0'}, use_global_device_ids=true, to_apply=%region_4.5 | all-reduce | flops 8256 | bytes 66048 | tf_op jit(solution)/shard_map/psum | solution.py:37
  90.3 11.9 %all-reduce.1 = (f32[64]{0:T(128)S(1)}, f32[64,128]{1,0:T(8,128)S(1)}) all-reduce(f32[64]{0:T(128)S(1)} %get-tuple-element.6, f32[64,128]{1,0:T(8,128)S(1)} %get-tuple-element.7), channel_id=1, replica_groups=mesh['lon_0'=4,'lon_1'=4,'lat'=8,'mem'=2] {'lon_1'}, use_global_device_ids=true, to_apply=%region_5.6 | all-reduce | flops 8256 | bytes 66048 | tf_op jit(solution)/shard_map/psum | solution.py:37
  102.4 21.2 %all-reduce = (f32[64,1]{1,0:T(8,128)S(1)}, f32[64,128]{1,0:T(8,128)S(1)}) all-reduce(f32[64,1]{1,0:T(8,128)S(1)} %copy.74, f32[64,128]{1,0:T(8,128)S(1)} %get-tuple-element.5), channel_id=1, replica_groups=mesh['lon_0'=4,'lon_1'=4,'lat'=8,'mem'=2] {'lat'}, use_global_device_ids=true, to_apply=%region_6.7 | all-reduce | flops 8256 | bytes 66048 | tf_op jit(solution)/shard_map/psum | solution.py:37
  123.6 21.1 %all_gather.11 = f32[128,129]{1,0:T(8,128)S(1)} all-gather(f32[64,129]{1,0:T(8,128)S(1)} %pad_maximum_fusion.5), channel_id=1, replica_groups=mesh['lon_0'=4,'lon_1'=4,'lat'=8,'mem'=2] {'mem'}, dimensions={0}, use_global_device_ids=true | all-gather | bytes 99072 | tf_op jit(solution)/shard_map/all_gather | solution.py:46
  145.5 0.8 fusion.50
  146.4 0.9 fusion.96
  152.9 4.2 %reshape.129 = bf16[3,128,4096]{2,1,0:T(8,128)(2,1)S(1)} reshape(bf16[3,128,16,256]{3,2,1,0:T(8,128)(2,1)} %all-gather.3.cloned.1.call-done) | data formatting | bytes 6291456 | tf_op jit(solution)/shard_map/reshape | solution.py:196
  157.1 2.3 %fusion.5 = bf16[3,64,4096]{2,1,0:T(8,128)(2,1)S(1)} fusion(bf16[3,128,4096]{2,1,0:T(8,128)(2,1)S(1)} %reshape.129, bf16[2,64,4096]{2,1,0:T(8,128)(2,1)} %concatenate.39, bf16[1,64,4096]{2,1,0:T(8,128)(2,1)} %concatenate.38, f32[4096]{0:T(1024)S(1)} %bitcast.210, f32[128,128]{0,1:T(8,128)S(1)} %convolution_divide_fusion, s32[]{:T(128)S(6)} %select_n.47), kind=kOutput, calls=%fused_computation.7 | convolution fusion | flops 206061568 | bytes 6340612 | tf_op jit(solution)/shard_map/nk,snc->skc/dot_general | solution.py:197
  159.4 1.6 copy.87
  (108 shorter events, 16.0 us)
Async XLA Ops:
  7.2 10.8 %copy-start.5 = (f32[128,64]{0,1:T(8,128)S(1)}, f32[128,64]{0,1:T(8,128)}, u32[]{:S(2)}) copy-start(f32[128,64]{0,1:T(8,128)} %param.20) | copy-start | bytes 98308
  7.2 10.7 %copy-start.8 = (s32[128]{0:T(128)S(1)}, s32[128]{0:T(128)}, u32[]{:S(2)}) copy-start(s32[128]{0:T(128)} %param.23) | copy-start | bytes 1540
  7.2 10.8 %copy-start.9 = (s32[128,1]{0,1:T(1,128)S(1)}, s32[128,1]{0,1:T(1,128)}, u32[]{:S(2)}) copy-start(s32[128,1]{0,1:T(1,128)} %param.22) | copy-start | bytes 1540
  7.2 10.9 %copy-start.6 = (s32[128,64]{0,1:T(8,128)S(1)}, s32[128,64]{0,1:T(8,128)}, u32[]{:S(2)}) copy-start(s32[128,64]{0,1:T(8,128)} %param.21) | copy-start | bytes 98308
  7.2 70.0 %all-gather.5.cloned.1.call-start = ((), (), s32[]{:S(2)}) async-start(), calls=%async_computation.2 | async-start | bytes 1572864 | tf_op jit(solution)/shard_map/all_gather | solution.py:172
  11.7 6.9 %collective-permute-start = (bf16[68,16,4]{0,1,2:T(8,128)(2,1)S(1)}, bf16[68,16,4]{0,1,2:T(8,128)(2,1)S(1)}, u32[]{:S(2)}, u32[]{:S(2)}) collective-permute-start(bf16[68,16,4]{0,1,2:T(8,128)(2,1)S(1)} %copy.67), channel_id=1, source_target_pairs={{0,16},{16,32},{32,48},{48,64},{64,80},{80,96},{96,112},{112,128},... | collective-permute-start | bytes 26120 | tf_op jit(solution)/shard_map/ppermute | solution.py:22
  14.1 4.8 %collective-permute-start.1 = (bf16[68,16,4]{0,1,2:T(8,128)(2,1)S(1)}, bf16[68,16,4]{0,1,2:T(8,128)(2,1)S(1)}, u32[]{:S(2)}, u32[]{:S(2)}) collective-permute-start(bf16[68,16,4]{0,1,2:T(8,128)(2,1)S(1)} %copy.68), channel_id=1, source_target_pairs={{16,0},{32,16},{48,32},{64,48},{80,64},{96,80},{112,96},{128,112},... | collective-permute-start | bytes 26120 | tf_op jit(solution)/shard_map/ppermute | solution.py:23
  19.9 6.3 %collective-permute-start.2 = (bf16[68,4,264]{2,1,0:T(4,128)(2,1)S(1)}, bf16[68,4,264]{2,1,0:T(4,128)(2,1)S(1)}, u32[]{:S(2)}, u32[]{:S(2)}) collective-permute-start(bf16[68,4,264]{2,1,0:T(4,128)(2,1)S(1)} %get-tuple-element.34), channel_id=1, source_target_pairs={{0,2},{2,4},{4,6},{6,8},{8,10},{10,12},{12,14},{1,3},{3,5},{5,7},{... | collective-permute-start | bytes 430856 | tf_op jit(solution)/shard_map/ppermute | solution.py:22
  23.5 6.7 %collective-permute-start.3 = (bf16[68,4,264]{2,1,0:T(4,128)(2,1)S(1)}, bf16[68,4,264]{2,1,0:T(4,128)(2,1)S(1)}, u32[]{:S(2)}, u32[]{:S(2)}) collective-permute-start(bf16[68,4,264]{2,1,0:T(4,128)(2,1)S(1)} %get-tuple-element.35), channel_id=1, source_target_pairs={{2,0},{4,2},{6,4},{8,6},{10,8},{12,10},{14,12},{3,1},{5,3},{7,5},{... | collective-permute-start | bytes 430856 | tf_op jit(solution)/shard_map/ppermute | solution.py:23
  41.2 35.6 %copy-start.1 = (f32[65,16,256]{2,1,0:T(8,128)}, f32[65,16,256]{2,1,0:T(8,128)S(1)}, u32[]{:S(2)}) copy-start(f32[65,16,256]{2,1,0:T(8,128)S(1)} %fusion.56) | copy-start | bytes 3194884
  41.3 1.2 copy-start.7
  42.4 17.0 %copy-start.3 = (s32[16,256]{1,0:T(8,128)S(1)}, s32[16,256]{1,0:T(8,128)}, u32[]{:S(2)}) copy-start(s32[16,256]{1,0:T(8,128)} %param.18) | copy-start | bytes 49156
  42.4 17.1 %copy-start.2 = (bf16[2,64,16,256]{3,2,1,0:T(8,128)(2,1)S(1)}, bf16[2,64,16,256]{3,2,1,0:T(8,128)(2,1)}, u32[]{:S(2)}) copy-start(bf16[2,64,16,256]{3,2,1,0:T(8,128)(2,1)} %param.14) | copy-start | bytes 3145732
  44.7 26.5 %all-to-all-start = ((f32[128,1,384]{2,1,0:T(1,128)}), f32[128,1,384]{2,1,0:T(1,128)S(1)}, u32[]{:S(2)}, u32[]{:S(2)}) async-start(f32[128,1,384]{2,1,0:T(1,128)} %reshape.150), calls=%async_computation | async-start | bytes 393216 | tf_op jit(solution)/shard_map/all_to_all | solution.py:31
  59.4 93.5 %all-gather.3.cloned.1.call-start = ((), (), s32[]{:S(2)}) async-start(), calls=%async_computation.1 | async-start | bytes 4718592 | tf_op jit(solution)/shard_map/all_gather | solution.py:194
  73.9 3.1 %copy-start = (bf16[8,8,16,256]{3,1,2,0:T(8,128)(2,1)S(1)}, bf16[8,8,16,256]{3,1,2,0:T(8,128)(2,1)}, u32[]{:S(2)}) copy-start(bf16[8,8,16,256]{3,1,2,0:T(8,128)(2,1)} %copy.84) | copy-start | bytes 1572868
  159.4 2.1 %slice-start = ((f32[65,16,256]{2,1,0:T(8,128)}), f32[1,16,256]{2,1,0:T(8,128)S(1)}, s32[]{:S(2)}) async-start(f32[65,16,256]{2,1,0:T(8,128)} %copy-done.1), calls=%async_computation.3 | async-start | bytes 32768 | tf_op jit(solution)/shard_map/slice | solution.py:125
  159.4 2.1 %copy-start.4 = (f32[2,16,256]{2,1,0:T(8,128)S(1)}, f32[2,16,256]{2,1,0:T(8,128)}, u32[]{:S(2)}) copy-start(f32[2,16,256]{2,1,0:T(8,128)} %param.15) | copy-start | bytes 98308
Sparse Core Ops, SparseCore 0:
  42.5 19.9 all-gather.4
  64.9 20.6 all-gather.2

commit v2 on v0

v2 whole, which is shorter than its diff:
```python
import functools

import jax
import jax.numpy as jnp
from jax import lax
from jax.experimental import pallas as pl
from jax.experimental.pallas import tpu as pltpu
from jax.sharding import PartitionSpec as P

SUBSTEPS = 4
NS_ITERS = 8
BF = jnp.bfloat16
F32 = jnp.float32
MESH_ID = pl.DeviceIdType.MESH
LIMIT = 48 * 1024 * 1024
NT = (((1,), (1,)), ((), ()))

LON_LAT = ("lon", "lat")
SIDES = ((1, 0), (-1, 0), (1, 1), (1, -1), (-1, 1), (-1, -1))


def iota(shape, dim):
    return lax.broadcasted_iota(jnp.int32, shape, dim)


def remote(src, dst, send, recv, where):
    return pltpu.make_async_remote_copy(
        src_ref=src,
        dst_ref=dst,
        send_sem=send,
        recv_sem=recv,
        device_id=where,
        device_id_type=MESH_ID,
    )


def spot(lon, lat, mem):
    return {"lon": lon, "lat": lat, "mem": mem}


def row_of_all(stage, r, members):
    half = members * 16
    parts = [stage[pl.ds(h * half + r, members, stride=16), :] for h in range(2)]
    return jnp.concatenate(parts, axis=1)


def greet(places):
    barrier = pltpu.get_barrier_semaphore()
    for place in places:
        pl.semaphore_signal(barrier, inc=1, device_id=place, device_id_type=MESH_ID)
    return barrier, len(places)


def exchange_kernel(
    nlon,
    nlat,
    anom,
    mean,
    cx,
    cy,
    ocean,
    values,
    variance,
    cells,
    tile,
    count,
    lagged,
    from_north,
    from_south,
    beside,
    field_north,
    field_south,
    field_beside,
    arrived,
    lag_all,
    to_south,
    to_north,
    edges,
    fields,
    field_edges,
    placed,
    midway,
    turned,
    lag_near,
    stage,
    lag_sem,
    halo_send,
    halo_recv,
    lat_send,
    lat_recv,
    lon_send,
    lon_recv,
):
    lon, lat, mem = lax.axis_index("lon"), lax.axis_index("lat"), lax.axis_index("mem")

    def at(dx, dy):
        return spot(lax.rem(lon + dx + nlon, nlon), lax.rem(lat + dy + nlat, nlat), mem)

    peers = [at(0, d) for d in range(1, nlat)] + [at(d, 0) for d in range(1, nlon)]
    peers += [at(dx, dy) for dx, dy in SIDES if dy != 0]
    twin = spot(lon, lat, 1 - mem)
    barrier, total = greet(peers + [twin])
    load = pltpu.make_async_copy(lagged, lag_near, lag_sem.at[0])
    load.start()

    half = anom.shape[0] // 2
    sub = iota((half, 8, 256), 1)
    top = anom[:, 0:8, :].astype(F32)
    low = jnp.where(sub < 4, top[:half], pltpu.roll(top[half:], 4, 1))
    to_south[...] = low.astype(BF)
    bottom = anom[:, 8:16, :].astype(F32)
    high = jnp.where(sub < 4, pltpu.roll(bottom[:half], 4, 1), bottom[half:])
    to_north[...] = high.astype(BF)
    fields[0] = mean[...]
    fields[1] = cx[...]
    fields[2] = cy[...]
    fields[3] = ocean[...].astype(F32)

    lane = iota((16, 128), 1)

    def both_edges(x):
        return jnp.where(lane < 64, x[:, 0:128], x[:, 128:256])

    def packed(member, number):
        out = jnp.zeros((16, 128), F32)
        for k in range(number):
            moved = pltpu.roll(both_edges(member(k)), 8 * k, 1) if k else both_edges(member(k))
            mine = ((lane + 4) % 128) // 8 == k
            out = jnp.where(mine, moved, out)
        return out

    field_edges[...] = packed(lambda k: fields[k], 4)
    for g in range(anom.shape[0] // 16):
        edges[g] = packed(lambda k: anom[16 * g + k].astype(F32), 16).astype(BF)

    pl.semaphore_wait(barrier, total)

    copies = [
        remote(to_south, from_north, halo_send.at[0], halo_recv.at[0], at(0, -1)),
        remote(to_north, from_south, halo_send.at[1], halo_recv.at[1], at(0, 1)),
        remote(
            fields.at[:, 0:8, :], field_north, halo_send.at[2], halo_recv.at[2], at(0, -1)
        ),
        remote(
            fields.at[:, 8:16, :], field_south, halo_send.at[3], halo_recv.at[3], at(0, 1)
        ),
    ]
    for i, (dx, dy) in enumerate(SIDES):
        copies.append(
            remote(
                edges, beside.at[i], halo_send.at[4 + i], halo_recv.at[4 + i], at(-dx, -dy)
            )
        )
        copies.append(
            remote(
                field_edges,
                field_beside.at[i],
                halo_send.at[10 + i],
                halo_recv.at[10 + i],
                at(-dx, -dy),
            )
        )
    for copy in copies:
        copy.start()

    blocks, slots = values.shape
    row_i, col_i = iota((blocks, blocks), 0), iota((blocks, blocks), 1)
    same = row_i == col_i
    tile_col = jnp.broadcast_to(tile[...].astype(F32), (blocks, blocks))
    tile_row = jnp.sum(jnp.where(same, tile_col, 0.0), axis=0, keepdims=True)
    count_row = jnp.broadcast_to(count[...].astype(F32), (blocks, blocks))
    count_col = jnp.sum(jnp.where(same, count_row, 0.0), axis=1, keepdims=True)
    before = (tile_col == tile_row) & (row_i < col_i)
    rank = jnp.sum(jnp.where(before, 1.0, 0.0), axis=0, keepdims=True)
    wanted = (row_i % nlon) * nlat + row_i // nlon
    chosen = (wanted.astype(F32) == tile_row) & (rank == mem.astype(F32))
    selection = jnp.where(chosen, 1.0, 0.0).astype(BF)

    valid = iota((blocks, slots), 1).astype(F32) < count_col
    weight = jnp.where(valid, 1.0 / variance[...], 0.0)
    scaled = weight * values[...]
    where = cells[...]
    w_hi = weight.astype(BF).astype(F32)
    v_hi = scaled.astype(BF).astype(F32)
    payload = jnp.concatenate(
        [
            w_hi,
            weight - w_hi,
            v_hi,
            scaled - v_hi,
            (where // 256).astype(F32),
            (where % 256).astype(F32),
        ],
        axis=1,
    ).astype(BF)
    spread = jnp.dot(selection, payload, preferred_element_type=F32).astype(BF)
    placed[...] = spread.reshape(nlat, nlon, 6 * slots)

    first = []
    for d in range(1, nlat):
        to = lax.rem(lat + d, nlat)
        copy = remote(
            placed.at[to], midway.at[lat], lat_send.at[d - 1], lat_recv.at[d - 1], at(0, d)
        )
        copy.start()
        first.append(copy)
    midway[lat] = placed[lat]
    members = anom.shape[0]
    base = pl.multiple_of(mem * members, members)
    load.wait()
    for which in range(2):
        for h in range(2):
            part = lag_near[which, :, :, 128 * h : 128 * h + 128].astype(F32)
            stage[which, h * members * 16 : (h + 1) * members * 16] = part.reshape(-1, 128)
        for r in range(16):
            row = row_of_all(stage.at[which], r, members)
            lag_all[which, r, pl.ds(base, members), :] = row.astype(BF)
        copies.append(
            remote(
                lag_all.at[which, :, pl.ds(base, members), :],
                lag_all.at[which, :, pl.ds(base, members), :],
                halo_send.at[16 + which],
                halo_recv.at[16 + which],
                twin,
            )
        )
        copies[-1].start()
    for copy in first:
        copy.wait()

    swap = (row_i // nlat == col_i % nlon) & (row_i % nlat == col_i // nlon)
    mixed = midway[...].reshape(blocks, 6 * slots)
    ordered = jnp.dot(jnp.where(swap, 1.0, 0.0).astype(BF), mixed, preferred_element_type=F32)
    turned[...] = ordered.reshape(nlon, nlat, 6 * slots).astype(BF)
    second = []
    for d in range(1, nlon):
        to = lax.rem(lon + d, nlon)
        copy = remote(
            turned.at[to], arrived.at[lon], lon_send.at[d - 1], lon_recv.at[d - 1], at(d, 0)
        )
        copy.start()
        second.append(copy)
    arrived[lon] = turned[lon]
    for copy in second + copies:
        copy.wait()


def exchange(nlon, nlat, *args):
    members = args[0].shape[0]
    slots = args[5].shape[1]
    vm = pl.BlockSpec(memory_space=pltpu.VMEM)
    sds = jax.ShapeDtypeStruct
    lanes = 6 * slots
    return pl.pallas_call(
        functools.partial(exchange_kernel, nlon, nlat),
        out_shape=(
            sds((members // 2, 8, 256), BF),
            sds((members // 2, 8, 256), BF),
            sds((6, members // 16, 16, 128), BF),
            sds((4, 8, 256), F32),
            sds((4, 8, 256), F32),
            sds((6, 16, 128), F32),
            sds((nlon, nlat, lanes), BF),
            sds((2, 16, 2 * members, 256), BF),
        ),
        in_specs=[vm] * (len(args) - 1) + [pl.BlockSpec(memory_space=pl.ANY)],
        out_specs=(vm,) * 8,
        scratch_shapes=[
            pltpu.VMEM((members // 2, 8, 256), BF),
            pltpu.VMEM((members // 2, 8, 256), BF),
            pltpu.VMEM((members // 16, 16, 128), BF),
            pltpu.VMEM((4, 16, 256), F32),
            pltpu.VMEM((16, 128), F32),
            pltpu.VMEM((nlat, nlon, lanes), BF),
            pltpu.VMEM((nlat, nlon, lanes), BF),
            pltpu.VMEM((nlon, nlat, lanes), BF),
            pltpu.VMEM((2, members, 16, 256), BF),
            pltpu.VMEM((2, members * 32, 128), F32),
            pltpu.SemaphoreType.DMA((1,)),
            pltpu.SemaphoreType.DMA((18,)),
            pltpu.SemaphoreType.DMA((18,)),
            pltpu.SemaphoreType.DMA((nlat - 1,)),
            pltpu.SemaphoreType.DMA((nlat - 1,)),
            pltpu.SemaphoreType.DMA((nlon - 1,)),
            pltpu.SemaphoreType.DMA((nlon - 1,)),
        ],
        compiler_params=pltpu.CompilerParams(
            collective_id=0, has_side_effects=True, vmem_limit_bytes=LIMIT
        ),
        name="exchange",
    )(*args)


def forecast_kernel(
    nlat,
    anom,
    mean,
    cx,
    cy,
    ocean,
    from_north,
    from_south,
    beside,
    field_north,
    field_south,
    field_beside,
    arrived,
    rows_out,
    mean_out,
    cell_out,
    coef,
    side,
    stage,
    planes,
):
    lat = lax.axis_index("lat")
    members = anom.shape[0]
    half = members // 2
    north_ok = lat < nlat - 1
    south_ok = lat > 0
    lane16, sub8 = iota((16, 128), 1), iota((8, 128), 0)
    lane8 = iota((8, 128), 1)

    def sides(east, west, north_east, south_east, north_west, south_west):
        core = jnp.where(lane16 % 8 < 4, east, west)
        is_east = lane8 % 8 < 4
        up = jnp.where(is_east, north_east[0:8], north_west[0:8])
        down = jnp.where(is_east, south_east[8:16], south_west[8:16])
        up = jnp.where(north_ok, up, 0.0)
        down = jnp.where(south_ok, down, 0.0)
        return jnp.concatenate([core, jnp.where(sub8 < 4, up, down)], axis=0)

    for g in range(members // 16):
        side[g] = sides(*[beside[i, g].astype(F32) for i in range(6)])
    field_side = sides(*[field_beside[i] for i in range(6)])

    lane24 = iota((24, 128), 1)
    keep = (lane24 < 4) | (lane24 >= 124)
    subw = iota((8, 256), 0)

    def whole(core, up, down, turned):
        outer = jnp.where(subw < 4, jnp.where(north_ok, up, 0.0), jnp.where(south_ok, down, 0.0))
        return jnp.concatenate([jnp.concatenate([core, outer], axis=0), turned], axis=1)

    extended = []
    for k, core in enumerate((mean[...], cx[...], cy[...], ocean[...].astype(F32))):
        turned = pltpu.roll(field_side, 128 - 8 * k, 1) if k else field_side
        turned = jnp.where(keep, turned, 0.0)
        extended.append(whole(core, field_north[k], field_south[k], turned))
    ex_mean, ex_x, ex_y, ex_wet = extended
    coef[0] = ex_wet * jnp.maximum(ex_x, 0.0)
    coef[1] = -ex_wet * jnp.minimum(ex_x, 0.0)
    coef[2] = ex_wet * jnp.maximum(ex_y, 0.0)
    coef[3] = -ex_wet * jnp.minimum(ex_y, 0.0)

    def advance(q):
        for _ in range(SUBSTEPS):
            west = pltpu.roll(q, 1, 1)
            east = pltpu.roll(q, q.shape[1] - 1, 1)
            south = pltpu.roll(q, 1, 0)
            north = pltpu.roll(q, q.shape[0] - 1, 0)
            q = (
                q
                + coef[0] * (west - q)
                + coef[1] * (east - q)
                + coef[2] * (south - q)
                + coef[3] * (north - q)
            )
        return q[0:16, 0:256]

    mean_out[...] = advance(ex_mean)

    def one(i, carry):
        north, south = from_north[i].astype(F32), from_south[i].astype(F32)
        for second in (False, True):
            m = i + half if second else i
            up = pltpu.roll(north, 4, 0) if second else north
            down = south if second else pltpu.roll(south, 4, 0)
            turn = lax.rem(128 - 8 * lax.rem(i, 16), 128)
            turned = pltpu.roll(side[m // 16], turn, 1)
            q = whole(anom[m].astype(F32), up, down, turned)
            moved = advance(q)
            for h in range(2):
                start = pl.multiple_of((h * members + m) * 16, 16)
                stage[pl.ds(start, 16), :] = moved[:, 128 * h : 128 * h + 128]
        return carry

    lax.fori_loop(0, half, one, 0)
    for r in range(16):
        rows_out[r] = row_of_all(stage, r, members).astype(BF)

    lanes = arrived.shape[2]
    table = arrived[...].astype(F32).reshape(-1, lanes)
    count = table.shape[0] // 2
    first = iota((count, 128), 1) < 64
    for j in range(3):
        a = table[0:count, 128 * j : 128 * (j + 1)]
        b = table[count : 2 * count, 128 * j : 128 * (j + 1)]
        planes[2 * j] = jnp.where(first, a, pltpu.roll(b, 64, 1))
        planes[2 * j + 1] = jnp.where(first, pltpu.roll(a, 64, 1), b)
    row_id = iota((16, 256), 0).astype(F32)
    col_id = iota((256, 256), 0).astype(F32)

    def histogram(s, acc):
        def wide(p):
            return jnp.concatenate(
                [planes[p, pl.ds(2 * s, 1), :], planes[p, pl.ds(2 * s + 1, 1), :]], axis=1
            )

        hit = row_id == wide(4)
        left = jnp.concatenate([jnp.where(hit, wide(p), 0.0) for p in range(4)], axis=0)
        right = jnp.where(col_id == wide(5), 1.0, 0.0)
        return acc + lax.dot_general(
            left.astype(BF), right.astype(BF), NT, preferred_element_type=F32
        )

    acc = lax.fori_loop(0, count // 2, histogram, jnp.zeros((64, 256), F32))
    cell_out[0:16] = acc[0:16] + acc[16:32]
    cell_out[16:32] = acc[32:48] + acc[48:64]


def forecast(nlat, *args):
    members = args[0].shape[0]
    vm = pl.BlockSpec(memory_space=pltpu.VMEM)
    sds = jax.ShapeDtypeStruct
    return pl.pallas_call(
        functools.partial(forecast_kernel, nlat),
        out_shape=(
            sds((16, members, 256), BF),
            sds((16, 256), F32),
            sds((32, 256), F32),
        ),
        in_specs=[vm] * len(args),
        out_specs=(vm,) * 3,
        scratch_shapes=[
            pltpu.VMEM((4, 24, 384), F32),
            pltpu.VMEM((members // 16, 24, 128), F32),
            pltpu.VMEM((members * 32, 128), F32),
            pltpu.VMEM((6, 64, 128), F32),
        ],
        compiler_params=pltpu.CompilerParams(vmem_limit_bytes=LIMIT),
        name="forecast",
    )(*args)


def gram_kernel(
    nlon,
    nlat,
    own,
    cell,
    mean,
    everyone,
    gram,
    projection,
    cell_other,
    left,
    parts,
    got_lat,
    mine,
    got_lon,
    pair_send,
    pair_recv,
    lat_send,
    lat_recv,
    lon_send,
    lon_recv,
    all_send,
    all_recv,
):
    lon, lat, mem = lax.axis_index("lon"), lax.axis_index("lat"), lax.axis_index("mem")
    members = own.shape[1]
    base = pl.multiple_of(mem * members, members)
    twin = spot(lon, lat, 1 - mem)

    def at(dx, dy, m):
        return spot(lax.rem(lon + dx, nlon), lax.rem(lat + dy, nlat), m)

    across = [(d, m) for m in (0, 1) for d in range(nlat) if d or m]
    peers = [at(d, 0, mem) for d in range(1, nlon)]
    peers += [at(0, d, mem + m - 2 * mem * m) for d, m in across]
    barrier, total = greet(peers)
    everyone[:, pl.ds(base, members), :] = own[...]
    pl.semaphore_wait(barrier, total)

    pair = [
        remote(cell, cell_other, pair_send.at[0], pair_recv.at[0], twin),
        remote(
            own,
            everyone.at[:, pl.ds(base, members), :],
            pair_send.at[1],
            pair_recv.at[1],
            twin,
        ),
    ]
    for copy in pair:
        copy.start()
    pair[0].wait()
    sums = cell[...] + cell_other[...]
    weight = sums[0:16]
    misfit = sums[16:32] - weight * mean[...]
    for r in range(16):
        x = own[r].astype(F32)
        left[r, 0:members] = (x * weight[r : r + 1]).astype(BF)
        left[r, members : members + 16] = jnp.broadcast_to(misfit[r : r + 1], (16, 256)).astype(BF)
    pair[1].wait()
    acc = jnp.zeros((members + 16, 2 * members), F32)
    for r in range(16):
        acc = acc + lax.dot_general(left[r], everyone[r], NT, preferred_element_type=F32)
    for z in range(nlat):
        parts[z, 0:8] = acc[8 * z : 8 * z + 8]
        parts[z, 8:16] = acc[members : members + 8]

    first = []
    for d in range(1, nlat):
        to = lax.rem(lat + d, nlat)
        copy = remote(
            parts.at[to], got_lat.at[lat], lat_send.at[d - 1], lat_recv.at[d - 1], at(0, d, mem)
        )
        copy.start()
        first.append(copy)
    got_lat[lat] = parts[lat]
    for copy in first:
        copy.wait()
    part = got_lat[0]
    for z in range(1, nlat):
        part = part + got_lat[z]
    mine[...] = part

    second = []
    for d in range(1, nlon):
        copy = remote(mine, got_lon.at[lon], lon_send.at[d - 1], lon_recv.at[d - 1], at(d, 0, mem))
        copy.start()
        second.append(copy)
    got_lon[lon] = part
    for copy in second:
        copy.wait()
    part = got_lon[0]
    for x in range(1, nlon):
        part = part + got_lon[x]
    projection[...] = part[8:16]
    slot = mem * nlat + lat
    gram[slot] = part[0:8]
    third = []
    for i, (d, m) in enumerate(across):
        copy = remote(
            gram.at[slot],
            gram.at[slot],
            all_send.at[i],
            all_recv.at[i],
            at(0, d, mem + m - 2 * mem * m),
        )
        copy.start()
        third.append(copy)
    for copy in third:
        copy.wait()


def gram_sum(nlon, nlat, own, cell, mean):
    members = own.shape[1]
    vm = pl.BlockSpec(memory_space=pltpu.VMEM)
    sds = jax.ShapeDtypeStruct
    return pl.pallas_call(
        functools.partial(gram_kernel, nlon, nlat),
        out_shape=(
            sds((16, 2 * members, 256), BF),
            sds((2 * nlat, 8, 2 * members), F32),
            sds((8, 2 * members), F32),
        ),
        in_specs=[vm] * 3,
        out_specs=(vm,) * 3,
        scratch_shapes=[
            pltpu.VMEM((32, 256), F32),
            pltpu.VMEM((16, members + 16, 256), BF),
            pltpu.VMEM((nlat, 16, 2 * members), F32),
            pltpu.VMEM((nlat, 16, 2 * members), F32),
            pltpu.VMEM((16, 2 * members), F32),
            pltpu.VMEM((nlon, 16, 2 * members), F32),
            pltpu.SemaphoreType.DMA((2,)),
            pltpu.SemaphoreType.DMA((2,)),
            pltpu.SemaphoreType.DMA((nlat - 1,)),
            pltpu.SemaphoreType.DMA((nlat - 1,)),
            pltpu.SemaphoreType.DMA((nlon - 1,)),
            pltpu.SemaphoreType.DMA((nlon - 1,)),
            pltpu.SemaphoreType.DMA((2 * nlat - 1,)),
            pltpu.SemaphoreType.DMA((2 * nlat - 1,)),
        ],
        compiler_params=pltpu.CompilerParams(
            collective_id=1, has_side_effects=True, vmem_limit_bytes=LIMIT
        ),
        name="gram_sum",
    )(own, cell, mean)


def product(a, b):
    a_hi, b_hi = a.astype(BF), b.astype(BF)
    a_lo = (a - a_hi.astype(F32)).astype(BF)
    b_lo = (b - b_hi.astype(F32)).astype(BF)
    lhs = jnp.concatenate([a_hi, a_hi, a_lo], axis=1)
    rhs = jnp.concatenate([b_hi, b_lo, b_hi], axis=0)
    return jnp.dot(lhs, rhs, preferred_element_type=F32)


def inverse_root(gram, projection):
    n = gram.shape[0]
    identity = (iota((n, n), 0) == iota((n, n), 1)).astype(F32)
    system = (n - 1.0) * identity + 0.5 * (gram + gram.T)
    sums = jnp.sum(jnp.abs(system), axis=1, keepdims=True)
    bound = jnp.max(sums, axis=0, keepdims=True)
    iterate = system / bound
    factor = 1.5 * identity - 0.5 * iterate
    iterate = product(iterate, factor)
    accum = factor
    for _ in range(NS_ITERS - 2):
        factor = 1.5 * identity - 0.5 * product(accum, iterate)
        both = product(jnp.concatenate([iterate, accum], axis=0), factor)
        iterate, accum = both[0:n], both[n:]
    factor = 1.5 * identity - 0.5 * product(accum, iterate)
    root = product(factor, accum) / jnp.sqrt(bound)
    inner = jnp.sum(root * projection, axis=1, keepdims=True)
    weights = jnp.sum(root * inner, axis=0, keepdims=True)
    return root, weights


def analysis_kernel(
    gram,
    projection,
    now,
    lag,
    ocean,
    mean,
    lag_means,
    out,
    mean_out,
    transform,
    left,
    stage,
):
    step = pl.program_id(0)
    mem = lax.axis_index("mem")
    members = now.shape[1]
    own = members // 2
    base = pl.multiple_of(mem * own, own)

    @pl.when(step == 0)
    def _():
        n = members
        root, weights = inverse_root(gram[...].reshape(n, n), projection[0:1])
        transform[...] = jnp.sqrt(n - 1.0) * root
        left[0:own] = transform[pl.ds(base, own), :].astype(BF)
        left[own : own + 16] = jnp.broadcast_to(weights, (16, n)).astype(BF)

    wet = ocean[...].astype(F32)

    def update(x, own_x, r, mean_row):
        moved = jnp.dot(left[...], x, preferred_element_type=F32)
        s = own_x.astype(F32)
        w = wet[r : r + 1]
        blended = s + w * (moved[0:own] - s)
        for h in range(2):
            rows = pl.ds(h * own * 16 + r, own, stride=16)
            stage[rows, :] = blended[:, 128 * h : 128 * h + 128]
        mean_out[0, r : r + 1] = mean_row + w * moved[own : own + 1]

    @pl.when(step == 0)
    def _():
        for r in range(16):
            update(now[r], now[r, pl.ds(base, own), :], r, mean[r : r + 1])

    @pl.when(step > 0)
    def _():
        for r in range(16):
            update(lag[0, r], lag[0, r, pl.ds(base, own), :], r, lag_means[0, r : r + 1])

    for h in range(2):
        part = stage[h * own * 16 : (h + 1) * own * 16]
        out[0, :, :, 128 * h : 128 * h + 128] = part.reshape(own, 16, 128).astype(BF)


def analysis(gram, projection, now, lag, ocean, mean, lag_means):
    members = now.shape[1]
    own = members // 2
    vm = pl.BlockSpec(memory_space=pltpu.VMEM)
    sds = jax.ShapeDtypeStruct

    def lagged(s):
        return jnp.maximum(s - 1, 0)

    lag_spec = pl.BlockSpec((1, 16, members, 256), lambda s: (lagged(s), 0, 0, 0))
    return pl.pallas_call(
        analysis_kernel,
        grid=(3,),
        out_shape=(sds((3, own, 16, 256), BF), sds((3, 16, 256), F32)),
        in_specs=[vm, vm, vm, lag_spec, vm, vm]
        + [pl.BlockSpec((1, 16, 256), lambda s: (lagged(s), 0, 0))],
        out_specs=(
            pl.BlockSpec((1, own, 16, 256), lambda s: (s, 0, 0, 0)),
            pl.BlockSpec((1, 16, 256), lambda s: (s, 0, 0)),
        ),
        scratch_shapes=[
            pltpu.VMEM((members, members), F32),
            pltpu.VMEM((own + 16, members), BF),
            pltpu.VMEM((own * 32, 128), F32),
        ],
        compiler_params=pltpu.CompilerParams(vmem_limit_bytes=LIMIT),
        name="analysis",
    )(gram, projection, now, lag, ocean, mean, lag_means)


def body(
    nlon,
    nlat,
    anomalies,
    state_mean,
    delayed_deviation_pair,
    lagged_means,
    courant_lon,
    courant_lat,
    ocean,
    obs_values,
    obs_variance,
    obs_cells,
    obs_tile,
    obs_count,
):
    grids = (anomalies, state_mean, courant_lon, courant_lat, ocean)
    *halos, arrived, lag = exchange(
        nlon,
        nlat,
        *grids,
        obs_values,
        obs_variance,
        obs_cells,
        obs_tile,
        obs_count.reshape(1, -1),
        delayed_deviation_pair,
    )
    own, prior_mean, cell = forecast(nlat, *grids, *halos, arrived)
    now, gram, projection = gram_sum(nlon, nlat, own, cell, prior_mean)
    return analysis(gram, projection, now, lag, ocean, prior_mean, lagged_means)


def solution(mesh):
    return jax.shard_map(
        functools.partial(body, mesh.shape["lon"], mesh.shape["lat"]),
        mesh=mesh,
        in_specs=(
            P("mem", "lat", "lon"),
            P("lat", "lon"),
            P(None, "mem", "lat", "lon"),
            P(None, "lat", "lon"),
            P("lat", "lon"),
            P("lat", "lon"),
            P("lat", "lon"),
            P(LON_LAT, None),
            P(LON_LAT, None),
            P(LON_LAT, None),
            P(LON_LAT, None),
            P(LON_LAT),
        ),
        out_specs=(P(None, "mem", "lat", "lon"), P(None, "lat", "lon")),
        check_vma=False,
    )
```

time: 340 us -> 84.9 us (0.25)
  local copies, waits for them, and re-layouts: 171 us -> 9.12 us
  Pallas kernels: 0 us -> 74.4 us
  blocking collectives: 69.6 us -> 0 us
  other arithmetic: 31.2 us -> 0 us
  starting transfers between devices: 27.7 us -> 0 us
  matrix products: 24 us -> 0 us
  between operations: 15.4 us -> 0.72 us
    gather x2 -> x0, local copies, waits for them, and re-layouts: 148 us -> none  [the longest x1 90.5 us: body(): prior_mean.reshape(-1)[grid_cells]]
    pallas_call x0 -> x4, Pallas kernels: none -> 74.4 us  [the longest x1 25.8 us: gram_sum(): pl.pallas_call(functools.partial(gram_kernel, nlon, nlat), out_shape=(sds...]
    psum x3 -> x0, blocking collectives: 50.1 us -> none  [over_axes(): x = lax.psum(x, axis)]
    dot_general x30 -> x0, matrix products: 24 us -> none  [the longest x1 9.73 us: body(): lax.dot_general(weighted, observed_all, (((0,), (0,)), ((), ())), preferr...]
    all_gather x1 -> x0, blocking collectives: 19.4 us -> none  [side_by_side(): out = lax.all_gather(both, axis, axis=dim, tiled=True)]
    all_to_all x1 -> x0, starting transfers between devices: 16.5 us -> none  [sent_together(): lax.all_to_all(both, axis, split_axis=split_dim, concat_axis=concat_dim,...]
    select_n x3 -> x0, other arithmetic: 11.6 us -> none  [the longest x2 11.6 us: body(): observed = jnp.take(cell_table, grid_cells, axis=0)]
    ppermute x4 -> x0, starting transfers between devices: 10.7 us -> none  [the longest x2 5.65 us: with_halo(): before = lax.ppermute(last, axis, up)]
  transfers between devices with their start and end apart: 7 -> 0, of which waited for: 0 -> 0; matrix products, arithmetic and copies ran while one was open for 58% -> 0% of each run, Pallas kernels for 0% -> 0%
where the time goes in v2:
time: 84.9 us; the launch traced here: 84.3 us
  Pallas kernels  74.4 us (88%)
  local copies, waits for them, and re-layouts  9.12 us (11%)
    pallas_call x1, Pallas kernels, gram_sum(): pl.pallas_call(functools.partial(gram_kernel, nlon, nlat), out_shape=(sds...  25.8 us
    pallas_call x1, Pallas kernels, exchange(): pl.pallas_call(functools.partial(exchange_kernel, nlon, nlat), out_shape=...  22.6 us
    pallas_call x1, Pallas kernels, forecast(): pl.pallas_call(functools.partial(forecast_kernel, nlat), out_shape=(sds((...  20.3 us
    unnamed x22, local copies, waits for them, and re-layouts  9.12 us
    pallas_call x1, Pallas kernels, analysis(): pl.pallas_call(analysis_kernel, grid=(3,), out_shape=(sds((3, own, 16, 25...  5.67 us

profile of v2, /device:TPU:1, one launch (start us, length us, event | category | flops | bytes accessed | tf_op | source)
XLA Modules:
  0.0 84.3 jit_solution(27148897927328947)
XLA Ops:
  0.6 0.0 copy-start.3
  0.6 0.0 copy-start.7
  0.7 0.9 %copy.14.values = f32[128,64]{1,0:T(8,128)S(1)} copy(f32[128,64]{0,1:T(8,128)} %param.19) | data formatting | bytes 65536 | tf_op args[7]
  1.5 0.9 %copy.15.variance = f32[128,64]{1,0:T(8,128)S(1)} copy(f32[128,64]{0,1:T(8,128)} %param.20) | data formatting | bytes 65536 | tf_op args[8]
  2.4 0.9 %copy.16.cells = s32[128,64]{1,0:T(8,128)S(1)} copy(s32[128,64]{0,1:T(8,128)} %param.21) | data formatting | bytes 65536 | tf_op args[9]
  3.2 0.8 copy.17.tile
  4.0 0.0 copy-start
  4.0 1.0 %copy-done = bf16[64,16,256]{2,1,0:T(8,128)(2,1)S(1)} copy-done((bf16[64,16,256]{2,1,0:T(8,128)(2,1)S(1)}, bf16[64,16,256]{2,1,0:T(8,128)(2,1)}, u32[]{:S(2)}) %copy-start) | copy-done | bytes 524312
  5.0 0.0 copy-start.1
  5.0 1.2 %copy-done.1 = bf16[2,64,16,256]{3,2,1,0:T(8,128)(2,1)S(1)} copy-done((bf16[2,64,16,256]{3,2,1,0:T(8,128)(2,1)S(1)}, bf16[2,64,16,256]{3,2,1,0:T(8,128)(2,1)}, u32[]{:S(2)}) %copy-start.1) | copy-done | bytes 1048600
  6.3 0.0 copy-start.2
  6.3 0.7 copy-done.2
  7.0 0.0 copy-start.4
  7.0 0.7 copy-done.4
  7.7 0.0 copy-start.5
  7.7 0.7 copy-done.5
  8.4 0.0 copy-start.6
  8.4 0.7 copy-done.6
  9.1 0.0 copy-start.8
  9.1 0.7 copy-done.8
  9.8 22.6 %exchange.1 = (bf16[32,8,256]{2,1,0:T(8,128)(2,1)S(1)}, bf16[32,8,256]{2,1,0:T(8,128)(2,1)S(1)}, bf16[6,4,16,128]{3,2,1,0:T(8,128)(2,1)S(1)}, f32[4,8,256]{2,1,0...) custom-call(bf16[64,16,256]{2,1,0:T(8,128)(2,1)S(1)} %copy-done, ...), custom_call_target="tpu_custom_call" | custom-call | tf_op jit(solution)/shard_map/exchange/pallas_call | solution.py:254
  32.4 20.3 %forecast.1 = (bf16[16,64,256]{2,1,0:T(8,128)(2,1)S(1)}, f32[16,256]{1,0:T(8,128)S(1)}, f32[32,256]{1,0:T(8,128)S(1)}) custom-call(bf16[64,16,256]{2,1,0:T(8,128)(2,1)S(1)} %copy-done, f32[16,256]{1,0:T(8,128)S(1)} %copy-done.4, f32[16,256]{1,0:T(8,128)S(1)} %copy-done.5, f32[16,256]{1,0:T(8,128)S(1)} %copy-done.6, s32[16,256]{1,0:T(8,128)S(1)} %copy-done.2, ...), custom_call_target="tpu_custom_call" | custom-call | tf_op jit(solution)/shard_map/forecast/pallas_call | solution.py:426
  52.8 25.8 %gram_sum.1 = (bf16[16,128,256]{2,1,0:T(8,128)(2,1)S(1)}, f32[16,8,128]{2,1,0:T(8,128)S(1)}, f32[8,128]{1,0:T(8,128)S(1)}) custom-call(bf16[16,64,256]{2,1,0:T(8,128)(2,1)S(1)} %get-tuple-element.23.own, f32[32,256]{1,0:T(8,128)S(1)} %get-tuple-element.24.cell, f32[16,256]{1,0:T(8,128)S(1)} %get-tuple-element.25.mean), custom_call_target="tpu_custom_call" | custom-call | tf_op jit(solution)/shard_map/gram_sum/pallas_call | solution.py:562
  78.6 0.0 copy-done.3
  78.6 0.0 copy-done.7
  78.6 5.7 %analysis.1 = (bf16[3,64,16,256]{3,2,1,0:T(8,128)(2,1)}, f32[3,16,256]{2,1,0:T(8,128)}) custom-call(f32[16,8,128]{2,1,0:T(8,128)S(1)} %get-tuple-element.26.gram, f32[8,128]{1,0:T(8,128)S(1)} %get-tuple-element.27.projection, bf16[16,128,256]{2,1,0:T(8,128)(2,1)S(1)} %get-tuple-element.28.now, bf16[2,16,128,256]{3,2,1,0:T(8,128)(2,1)S(1)} %get-tuple-element.29.lag, ...), custom_call_target="tpu_custom_call" | custom-call | tf_op jit(solution)/shard_map/analysis/pallas_call | solution.py:689
Async XLA Ops:
  0.6 78.0 %copy-start.3 = (s32[16,256]{1,0:T(8,128)S(1)}, s32[16,256]{1,0:T(8,128)}, u32[]{:S(2)}) copy-start(s32[16,256]{1,0:T(8,128)} %ocean.5) | copy-start | bytes 49156
  0.6 78.0 %copy-start.7 = (f32[2,16,256]{2,1,0:T(8,128)S(1)}, f32[2,16,256]{2,1,0:T(8,128)}, u32[]{:S(2)}) copy-start(f32[2,16,256]{2,1,0:T(8,128)} %lag_means.1) | copy-start | bytes 98308
  4.0 1.0 %copy-start = (bf16[64,16,256]{2,1,0:T(8,128)(2,1)S(1)}, bf16[64,16,256]{2,1,0:T(8,128)(2,1)}, u32[]{:S(2)}) copy-start(bf16[64,16,256]{2,1,0:T(8,128)(2,1)} %anom.3) | copy-start | bytes 1572868
  5.0 1.2 %copy-start.1 = (bf16[2,64,16,256]{3,2,1,0:T(8,128)(2,1)S(1)}, bf16[2,64,16,256]{3,2,1,0:T(8,128)(2,1)}, u32[]{:S(2)}) copy-start(bf16[2,64,16,256]{3,2,1,0:T(8,128)(2,1)} %lagged.1) | copy-start | bytes 3145732
  6.3 0.7 copy-start.2
  7.0 0.7 copy-start.4
  7.7 0.7 copy-start.5
  8.4 0.7 copy-start.6
  9.1 0.7 copy-start.8

commit v3 on v2

v3 whole, which is shorter than its diff:
```python
import functools

import jax
import jax.numpy as jnp
from jax import lax
from jax.experimental import pallas as pl
from jax.experimental.pallas import tpu as pltpu
from jax.sharding import PartitionSpec as P

SUBSTEPS = 4
NS_ITERS = 8
BF = jnp.bfloat16
F32 = jnp.float32
MESH_ID = pl.DeviceIdType.MESH
LIMIT = 48 * 1024 * 1024
NT = (((1,), (1,)), ((), ()))

LON_LAT = ("lon", "lat")
SIDES = ((1, 0), (-1, 0), (1, 1), (1, -1), (-1, 1), (-1, -1))


def iota(shape, dim):
    return lax.broadcasted_iota(jnp.int32, shape, dim)


def remote(src, dst, send, recv, where):
    return pltpu.make_async_remote_copy(
        src_ref=src,
        dst_ref=dst,
        send_sem=send,
        recv_sem=recv,
        device_id=where,
        device_id_type=MESH_ID,
    )


def spot(lon, lat, mem):
    return {"lon": lon, "lat": lat, "mem": mem}


def row_of_all(stage, r, members):
    half = members * 16
    parts = [stage[pl.ds(h * half + r, members, stride=16), :] for h in range(2)]
    return jnp.concatenate(parts, axis=1)


def greet(places):
    barrier = pltpu.get_barrier_semaphore()
    for place in places:
        pl.semaphore_signal(barrier, inc=1, device_id=place, device_id_type=MESH_ID)
    return barrier, len(places)


def smooth_kernel(
    nlon,
    nlat,
    anom_in,
    mean_in,
    cx_in,
    cy_in,
    ocean_in,
    values_in,
    variance_in,
    cells_in,
    tile_in,
    count_in,
    lagged_in,
    lag_means_in,
    everyone,
    gram,
    projection,
    mean_out,
    wet_out,
    lag_all,
    lag_means,
    anom,
    fields,
    ocean,
    values,
    variance,
    cells,
    tile,
    count,
    lag_near,
    to_south,
    to_north,
    edges,
    field_edges,
    from_north,
    from_south,
    beside,
    field_north,
    field_south,
    field_beside,
    placed,
    midway,
    turned,
    arrived,
    stage,
    coef,
    side,
    planes,
    cell,
    cell_other,
    left,
    parts,
    got_lat,
    mine,
    got_lon,
    load_sem,
    halo_send,
    halo_recv,
    chunk_send,
    chunk_recv,
    lat_send,
    lat_recv,
    lon_send,
    lon_recv,
    pair_send,
    pair_recv,
    sum_send,
    sum_recv,
    all_send,
    all_recv,
):
    lon, lat, mem = lax.axis_index("lon"), lax.axis_index("lat"), lax.axis_index("mem")
    twin = spot(lon, lat, 1 - mem)
    members = anom.shape[0]
    half = members // 2
    base = pl.multiple_of(mem * members, members)

    def at(dx, dy, m=mem):
        return spot(lax.rem(lon + dx + nlon, nlon), lax.rem(lat + dy + nlat, nlat), m)

    loads = [
        pltpu.make_async_copy(src, dst, load_sem.at[i])
        for i, (src, dst) in enumerate(
            (
                (anom_in, anom),
                (mean_in, fields.at[0]),
                (cx_in, fields.at[1]),
                (cy_in, fields.at[2]),
                (ocean_in, ocean),
                (tile_in, tile),
                (count_in, count),
                (values_in, values),
                (variance_in, variance),
                (cells_in, cells),
                (lagged_in, lag_near),
                (lag_means_in, lag_means),
            )
        )
    ]
    for load in loads:
        load.start()
    across = [(d, m) for m in (0, 1) for d in range(nlat) if d or m]

    def other(m):
        return mem + m - 2 * mem * m

    peers = [at(0, d, other(m)) for d, m in across]
    peers += [at(d, 0) for d in range(1, nlon)]
    peers += [at(dx, dy) for dx, dy in SIDES if dy != 0]
    barrier, total = greet(peers)

    for load in loads[:5]:
        load.wait()
    fields[3] = ocean[...].astype(F32)
    wet_out[...] = fields[3]
    sub = iota((half, 8, 256), 1)
    top = anom[:, 0:8, :].astype(F32)
    low = jnp.where(sub < 4, top[:half], pltpu.roll(top[half:], 4, 1))
    to_south[...] = low.astype(BF)
    bottom = anom[:, 8:16, :].astype(F32)
    high = jnp.where(sub < 4, pltpu.roll(bottom[:half], 4, 1), bottom[half:])
    to_north[...] = high.astype(BF)
    lane16 = iota((16, 128), 1)

    def both_edges(x):
        return jnp.where(lane16 < 64, x[:, 0:128], x[:, 128:256])

    def packed(member, number):
        out = jnp.zeros((16, 128), F32)
        for k in range(number):
            moved = pltpu.roll(both_edges(member(k)), 8 * k, 1) if k else both_edges(member(k))
            owner = ((lane16 + 4) % 128) // 8 == k
            out = jnp.where(owner, moved, out)
        return out

    field_edges[...] = packed(lambda k: fields[k], 4)
    for g in range(members // 16):
        edges[g] = packed(lambda k: anom[16 * g + k].astype(F32), 16).astype(BF)

    for load in loads[5:10]:
        load.wait()
    slots, blocks = values.shape
    row_i, col_i = iota((blocks, blocks), 0), iota((blocks, blocks), 1)
    tile_row = jnp.broadcast_to(tile[...].astype(F32), (blocks, blocks))
    tile_col = jnp.sum(jnp.where(row_i == col_i, tile_row, 0.0), axis=1, keepdims=True)
    before = (tile_col == tile_row) & (row_i < col_i)
    rank = jnp.sum(jnp.where(before, 1.0, 0.0), axis=0, keepdims=True)
    wanted = (row_i % nlon) * nlat + row_i // nlon
    chosen = (wanted.astype(F32) == tile_row) & (rank == mem.astype(F32))
    selection = jnp.where(chosen, 1.0, 0.0).astype(BF)
    valid = iota((slots, blocks), 0) < count[...]
    weight = jnp.where(valid, 1.0 / variance[...], 0.0)
    scaled = weight * values[...]
    where = cells[...]
    w_hi = weight.astype(BF).astype(F32)
    v_hi = scaled.astype(BF).astype(F32)
    payload = jnp.concatenate(
        [
            w_hi,
            weight - w_hi,
            v_hi,
            scaled - v_hi,
            (where // 256).astype(F32),
            (where % 256).astype(F32),
        ],
        axis=0,
    ).astype(BF)
    spread = lax.dot_general(selection, payload, NT, preferred_element_type=F32).astype(BF)
    placed[...] = spread.reshape(nlat, nlon, 6 * slots)

    pl.semaphore_wait(barrier, total)

    first = []
    for d in range(1, nlat):
        to = lax.rem(lat + d, nlat)
        first.append(
            remote(
                placed.at[to], midway.at[lat], lat_send.at[d - 1], lat_recv.at[d - 1], at(0, d)
            )
        )
    halo = []
    for i, (dx, dy) in enumerate(SIDES):
        there = at(-dx, -dy)
        halo.append(remote(edges, beside.at[i], halo_send.at[i], halo_recv.at[i], there))
        halo.append(
            remote(
                field_edges, field_beside.at[i], halo_send.at[6 + i], halo_recv.at[6 + i], there
            )
        )
    for j, (start, into, dy) in enumerate(((0, field_north, -1), (8, field_south, 1))):
        part = fields.at[:, pl.ds(start, 8), :]
        halo.append(remote(part, into, halo_send.at[12 + j], halo_recv.at[12 + j], at(0, dy)))
    chunks = 4
    wide_chunk = half // chunks
    bands = []
    for c in range(chunks):
        some = pl.ds(c * wide_chunk, wide_chunk)
        for j, (src, dst, dy) in enumerate(
            ((to_south, from_north, -1), (to_north, from_south, 1))
        ):
            k = 2 * c + j
            bands.append(
                remote(src.at[some], dst.at[some], chunk_send.at[k], chunk_recv.at[k], at(0, dy))
            )
    for copy in first + halo + bands:
        copy.start()
    midway[lat] = placed[lat]

    loads[10].wait()
    loads[11].wait()
    late = []
    for which in range(2):
        for h in range(2):
            part = lag_near[which, :, :, 128 * h : 128 * h + 128].astype(F32)
            stage[which, h * members * 16 : (h + 1) * members * 16] = part.reshape(-1, 128)
        for r in range(16):
            row = row_of_all(stage.at[which], r, members)
            lag_all[which, r, pl.ds(base, members), :] = row.astype(BF)
        ours = lag_all.at[which, :, pl.ds(base, members), :]
        late.append(remote(ours, ours, pair_send.at[5 + which], pair_recv.at[5 + which], twin))

    for copy in first:
        copy.wait()
    swap = (row_i // nlat == col_i % nlon) & (row_i % nlat == col_i // nlon)
    mixed = midway[...].reshape(blocks, 6 * slots)
    ordered = jnp.dot(jnp.where(swap, 1.0, 0.0).astype(BF), mixed, preferred_element_type=F32)
    turned[...] = ordered.reshape(nlon, nlat, 6 * slots).astype(BF)
    second = []
    for d in range(1, nlon):
        to = lax.rem(lon + d, nlon)
        copy = remote(
            turned.at[to], arrived.at[lon], lon_send.at[d - 1], lon_recv.at[d - 1], at(d, 0)
        )
        copy.start()
        second.append(copy)
    arrived[lon] = turned[lon]

    for copy in halo:
        copy.wait()
    north_ok = lat < nlat - 1
    south_ok = lat > 0
    sub8, lane8 = iota((8, 128), 0), iota((8, 128), 1)

    def sides(east, west, north_east, south_east, north_west, south_west):
        core = jnp.where(lane16 % 8 < 4, east, west)
        is_east = lane8 % 8 < 4
        up = jnp.where(is_east, north_east[0:8], north_west[0:8])
        down = jnp.where(is_east, south_east[8:16], south_west[8:16])
        up = jnp.where(north_ok, up, 0.0)
        down = jnp.where(south_ok, down, 0.0)
        return jnp.concatenate([core, jnp.where(sub8 < 4, up, down)], axis=0)

    for g in range(members // 16):
        side[g] = sides(*[beside[i, g].astype(F32) for i in range(6)])
    field_side = sides(*[field_beside[i] for i in range(6)])
    lane24 = iota((24, 128), 1)
    keep = (lane24 < 4) | (lane24 >= 124)
    subw = iota((8, 256), 0)

    def whole(core, up, down, turned):
        outer = jnp.where(subw < 4, jnp.where(north_ok, up, 0.0), jnp.where(south_ok, down, 0.0))
        return jnp.concatenate([jnp.concatenate([core, outer], axis=0), turned], axis=1)

    extended = []
    for k in range(4):
        turn = pltpu.roll(field_side, 128 - 8 * k, 1) if k else field_side
        turn = jnp.where(keep, turn, 0.0)
        extended.append(whole(fields[k], field_north[k], field_south[k], turn))
    ex_mean, ex_x, ex_y, ex_wet = extended
    coef[0] = ex_wet * jnp.maximum(ex_x, 0.0)
    coef[1] = -ex_wet * jnp.minimum(ex_x, 0.0)
    coef[2] = ex_wet * jnp.maximum(ex_y, 0.0)
    coef[3] = -ex_wet * jnp.minimum(ex_y, 0.0)
    coef[4] = 1.0 - ((coef[0] + coef[1]) + (coef[2] + coef[3]))

    def substep(q):
        west = pltpu.roll(q, 1, 1)
        east = pltpu.roll(q, q.shape[1] - 1, 1)
        south = pltpu.roll(q, 1, 0)
        north = pltpu.roll(q, q.shape[0] - 1, 0)
        return (coef[4] * q + coef[0] * west) + (coef[1] * east + coef[2] * south) + coef[3] * north

    q = ex_mean
    for _ in range(SUBSTEPS):
        q = substep(q)
    mean_out[...] = q[0:16, 0:256]
    together = 4

    def some_members(j, carry):
        where_to, group = [], []
        for k in range(together):
            i = j * together + k
            north, south = from_north[i].astype(F32), from_south[i].astype(F32)
            for second_half in (False, True):
                m = i + half if second_half else i
                up = pltpu.roll(north, 4, 0) if second_half else north
                down = south if second_half else pltpu.roll(south, 4, 0)
                turn = lax.rem(128 - 8 * lax.rem(i, 16), 128)
                turned_side = pltpu.roll(side[m // 16], turn, 1)
                where_to.append(m)
                group.append(whole(anom[m].astype(F32), up, down, turned_side))
        for _ in range(SUBSTEPS):
            group = [substep(q) for q in group]
        for m, q in zip(where_to, group):
            for h in range(2):
                start = pl.multiple_of((h * members + m) * 16, 16)
                stage[0, pl.ds(start, 16), :] = q[0:16, 128 * h : 128 * h + 128]
        return carry

    rounds = wide_chunk // together

    def advance(c):
        for copy in bands[2 * c : 2 * c + 2]:
            copy.wait()
        lax.fori_loop(c * rounds, (c + 1) * rounds, some_members, 0)

    for c in range(chunks - 1):
        advance(c)

    for copy in second:
        copy.wait()
    table = arrived[...].astype(F32).reshape(blocks, 6 * slots)
    pairs = blocks // 2
    near = iota((pairs, 128), 1) < 64
    for j in range(3):
        a = table[0:pairs, 128 * j : 128 * (j + 1)]
        b = table[pairs:blocks, 128 * j : 128 * (j + 1)]
        planes[2 * j] = jnp.where(near, a, pltpu.roll(b, 64, 1))
        planes[2 * j + 1] = jnp.where(near, pltpu.roll(a, 64, 1), b)
    row_id = iota((16, 256), 0).astype(F32)
    col_id = iota((256, 256), 0).astype(F32)

    def histogram(s, acc):
        def two(p):
            return jnp.concatenate(
                [planes[p, pl.ds(2 * s, 1), :], planes[p, pl.ds(2 * s + 1, 1), :]], axis=1
            )

        hit = row_id == two(4)
        lhs = jnp.concatenate([jnp.where(hit, two(p), 0.0) for p in range(4)], axis=0)
        rhs = jnp.where(col_id == two(5), 1.0, 0.0)
        return acc + lax.dot_general(lhs.astype(BF), rhs.astype(BF), NT, preferred_element_type=F32)

    acc = lax.fori_loop(0, pairs // 2, histogram, jnp.zeros((64, 256), F32), unroll=8)
    cell[0:16] = acc[0:16] + acc[16:32]
    cell[16:32] = acc[32:48] + acc[48:64]
    swap_cells = remote(cell, cell_other, pair_send.at[4], pair_recv.at[4], twin)
    swap_cells.start()

    advance(chunks - 1)

    swaps = []
    for c in range(4):
        for r in range(4 * c, 4 * c + 4):
            row = row_of_all(stage.at[0], r, members).astype(BF)
            everyone[r, pl.ds(base, members), :] = row
        ours = everyone.at[pl.ds(4 * c, 4), pl.ds(base, members), :]
        swaps.append(remote(ours, ours, pair_send.at[c], pair_recv.at[c], twin))
        swaps[-1].start()
    swap_cells.wait()
    sums = cell[...] + cell_other[...]
    weight = sums[0:16]
    misfit = sums[16:32] - weight * mean_out[...]
    for r in range(16):
        x = everyone[r, pl.ds(base, members), :].astype(F32)
        left[r, 0:members] = (x * weight[r : r + 1]).astype(BF)
        left[r, members : members + 16] = jnp.broadcast_to(misfit[r : r + 1], (16, 256)).astype(BF)
    acc = jnp.zeros((members + 16, 2 * members), F32)
    for c in range(4):
        swaps[c].wait()
        for r in range(4 * c, 4 * c + 4):
            acc = acc + lax.dot_general(left[r], everyone[r], NT, preferred_element_type=F32)
    for z in range(nlat):
        parts[z, 0:8] = acc[8 * z : 8 * z + 8]
        parts[z, 8:9] = acc[members : members + 1]

    first = []
    for d in range(1, nlat):
        to = lax.rem(lat + d, nlat)
        k = d - 1
        copy = remote(parts.at[to], got_lat.at[lat], sum_send.at[k], sum_recv.at[k], at(0, d))
        copy.start()
        first.append(copy)
    got_lat[lat] = parts[lat]
    for copy in late:
        copy.start()
    for copy in first:
        copy.wait()
    part = got_lat[0]
    for z in range(1, nlat):
        part = part + got_lat[z]
    mine[...] = part

    second = []
    for d in range(1, nlon):
        k = nlat + d - 2
        copy = remote(mine, got_lon.at[lon], sum_send.at[k], sum_recv.at[k], at(d, 0))
        copy.start()
        second.append(copy)
    got_lon[lon] = part
    for copy in second:
        copy.wait()
    part = got_lon[0]
    for x in range(1, nlon):
        part = part + got_lon[x]
    projection[...] = jnp.broadcast_to(part[8:9], projection.shape)
    slot = mem * nlat + lat
    gram[slot] = part[0:8]
    third = []
    for i, (d, m) in enumerate(across):
        copy = remote(
            gram.at[slot], gram.at[slot], all_send.at[i], all_recv.at[i], at(0, d, other(m))
        )
        copy.start()
        third.append(copy)
    for copy in third + late:
        copy.wait()


def smooth(nlon, nlat, *args):
    members = args[0].shape[0]
    slots, blocks = args[5].shape
    vm = pl.BlockSpec(memory_space=pltpu.VMEM)
    sds = jax.ShapeDtypeStruct
    lanes = 6 * slots
    pair = 2 * members
    dma = pltpu.SemaphoreType.DMA
    return pl.pallas_call(
        functools.partial(smooth_kernel, nlon, nlat),
        out_shape=(
            sds((16, pair, 256), BF),
            sds((2 * nlat, 8, pair), F32),
            sds((8, pair), F32),
            sds((16, 256), F32),
            sds((16, 256), F32),
            sds((2, 16, pair, 256), BF),
            sds((2, 16, 256), F32),
        ),
        in_specs=[pl.BlockSpec(memory_space=pltpu.MemorySpace.HBM)] * len(args),
        out_specs=(vm,) * 7,
        scratch_shapes=[
            pltpu.VMEM((members, 16, 256), BF),
            pltpu.VMEM((4, 16, 256), F32),
            pltpu.VMEM((16, 256), jnp.int32),
            pltpu.VMEM((slots, blocks), F32),
            pltpu.VMEM((slots, blocks), F32),
            pltpu.VMEM((slots, blocks), jnp.int32),
            pltpu.VMEM((1, blocks), jnp.int32),
            pltpu.VMEM((1, blocks), jnp.int32),
            pltpu.VMEM((2, members, 16, 256), BF),
            pltpu.VMEM((members // 2, 8, 256), BF),
            pltpu.VMEM((members // 2, 8, 256), BF),
            pltpu.VMEM((members // 16, 16, 128), BF),
            pltpu.VMEM((16, 128), F32),
            pltpu.VMEM((members // 2, 8, 256), BF),
            pltpu.VMEM((members // 2, 8, 256), BF),
            pltpu.VMEM((6, members // 16, 16, 128), BF),
            pltpu.VMEM((4, 8, 256), F32),
            pltpu.VMEM((4, 8, 256), F32),
            pltpu.VMEM((6, 16, 128), F32),
            pltpu.VMEM((nlat, nlon, lanes), BF),
            pltpu.VMEM((nlat, nlon, lanes), BF),
            pltpu.VMEM((nlon, nlat, lanes), BF),
            pltpu.VMEM((nlon, nlat, lanes), BF),
            pltpu.VMEM((2, members * 32, 128), F32),
            pltpu.VMEM((5, 24, 384), F32),
            pltpu.VMEM((members // 16, 24, 128), F32),
            pltpu.VMEM((6, blocks // 2, 128), F32),
            pltpu.VMEM((32, 256), F32),
            pltpu.VMEM((32, 256), F32),
            pltpu.VMEM((16, members + 16, 256), BF),
            pltpu.VMEM((nlat, 9, pair), F32),
            pltpu.VMEM((nlat, 9, pair), F32),
            pltpu.VMEM((9, pair), F32),
            pltpu.VMEM((nlon, 9, pair), F32),
            dma((12,)),
            dma((14,)),
            dma((14,)),
            dma((8,)),
            dma((8,)),
            dma((nlat - 1,)),
            dma((nlat - 1,)),
            dma((nlon - 1,)),
            dma((nlon - 1,)),
            dma((7,)),
            dma((7,)),
            dma((nlon + nlat - 2,)),
            dma((nlon + nlat - 2,)),
            dma((2 * nlat - 1,)),
            dma((2 * nlat - 1,)),
        ],
        compiler_params=pltpu.CompilerParams(
            collective_id=0, has_side_effects=True, vmem_limit_bytes=LIMIT
        ),
        name="smooth",
    )(*[pltpu.with_memory_space_constraint(a, pltpu.MemorySpace.HBM) for a in args])


def product(a, b):
    a_hi, b_hi = a.astype(BF), b.astype(BF)
    a_lo = (a - a_hi.astype(F32)).astype(BF)
    b_lo = (b - b_hi.astype(F32)).astype(BF)
    lhs = jnp.concatenate([a_hi, a_hi, a_lo], axis=1)
    rhs = jnp.concatenate([b_hi, b_lo, b_hi], axis=0)
    return jnp.dot(lhs, rhs, preferred_element_type=F32)


def inverse_root(gram, projection):
    n = gram.shape[0]
    identity = (iota((n, n), 0) == iota((n, n), 1)).astype(F32)
    system = (n - 1.0) * identity + 0.5 * (gram + gram.T)
    sums = jnp.sum(jnp.abs(system), axis=1, keepdims=True)
    bound = jnp.max(sums, axis=0, keepdims=True)
    iterate = system / bound
    factor = 1.5 * identity - 0.5 * iterate
    iterate = product(iterate, factor)
    accum = factor
    for _ in range(NS_ITERS - 2):
        factor = 1.5 * identity - 0.5 * product(accum, iterate)
        both = product(jnp.concatenate([iterate, accum], axis=0), factor)
        iterate, accum = both[0:n], both[n:]
    factor = 1.5 * identity - 0.5 * product(accum, iterate)
    root = product(factor, accum) / jnp.sqrt(bound)
    inner = jnp.sum(root * projection, axis=1, keepdims=True)
    weights = jnp.sum(root * inner, axis=0, keepdims=True)
    return root, weights


def analysis_kernel(
    gram,
    projection,
    now,
    lag,
    ocean,
    mean,
    lag_means,
    out,
    mean_out,
    transform,
    left,
    stage,
):
    step = pl.program_id(0)
    mem = lax.axis_index("mem")
    members = now.shape[1]
    own = members // 2
    base = pl.multiple_of(mem * own, own)

    @pl.when(step == 0)
    def _():
        n = members
        root, weights = inverse_root(gram[...].reshape(n, n), projection[0:1])
        transform[...] = jnp.sqrt(n - 1.0) * root
        left[0:own] = transform[pl.ds(base, own), :].astype(BF)
        left[own : own + 16] = jnp.broadcast_to(weights, (16, n)).astype(BF)

    wet = ocean[...]

    def update(x, own_x, r, mean_row):
        moved = jnp.dot(left[...], x, preferred_element_type=F32)
        s = own_x.astype(F32)
        w = wet[r : r + 1]
        blended = s + w * (moved[0:own] - s)
        for h in range(2):
            rows = pl.ds(h * own * 16 + r, own, stride=16)
            stage[rows, :] = blended[:, 128 * h : 128 * h + 128]
        mean_out[0, r : r + 1] = mean_row + w * moved[own : own + 1]

    @pl.when(step == 0)
    def _():
        for r in range(16):
            update(now[r], now[r, pl.ds(base, own), :], r, mean[r : r + 1])

    @pl.when(step > 0)
    def _():
        for r in range(16):
            update(lag[0, r], lag[0, r, pl.ds(base, own), :], r, lag_means[0, r : r + 1])

    for h in range(2):
        part = stage[h * own * 16 : (h + 1) * own * 16]
        out[0, :, :, 128 * h : 128 * h + 128] = part.reshape(own, 16, 128).astype(BF)


def analysis(gram, projection, now, lag, ocean, mean, lag_means):
    members = now.shape[1]
    own = members // 2
    vm = pl.BlockSpec(memory_space=pltpu.VMEM)
    sds = jax.ShapeDtypeStruct

    def lagged(s):
        return jnp.maximum(s - 1, 0)

    lag_spec = pl.BlockSpec((1, 16, members, 256), lambda s: (lagged(s), 0, 0, 0))
    return pl.pallas_call(
        analysis_kernel,
        grid=(3,),
        out_shape=(sds((3, own, 16, 256), BF), sds((3, 16, 256), F32)),
        in_specs=[vm, vm, vm, lag_spec, vm, vm]
        + [pl.BlockSpec((1, 16, 256), lambda s: (lagged(s), 0, 0))],
        out_specs=(
            pl.BlockSpec((1, own, 16, 256), lambda s: (s, 0, 0, 0)),
            pl.BlockSpec((1, 16, 256), lambda s: (s, 0, 0)),
        ),
        scratch_shapes=[
            pltpu.VMEM((members, members), F32),
            pltpu.VMEM((own + 16, members), BF),
            pltpu.VMEM((own * 32, 128), F32),
        ],
        compiler_params=pltpu.CompilerParams(vmem_limit_bytes=LIMIT),
        name="analysis",
    )(gram, projection, now, lag, ocean, mean, lag_means)


def body(
    nlon,
    nlat,
    anomalies,
    state_mean,
    delayed_deviation_pair,
    lagged_means,
    courant_lon,
    courant_lat,
    ocean,
    obs_values,
    obs_variance,
    obs_cells,
    obs_tile,
    obs_count,
):
    now, gram, projection, prior_mean, wet, lag, lag_means = smooth(
        nlon,
        nlat,
        anomalies,
        state_mean,
        courant_lon,
        courant_lat,
        ocean,
        obs_values.T,
        obs_variance.T,
        obs_cells.T,
        obs_tile.reshape(1, -1),
        obs_count.reshape(1, -1),
        delayed_deviation_pair,
        lagged_means,
    )
    return analysis(gram, projection, now, lag, wet, prior_mean, lag_means)


def solution(mesh):
    return jax.shard_map(
        functools.partial(body, mesh.shape["lon"], mesh.shape["lat"]),
        mesh=mesh,
        in_specs=(
            P("mem", "lat", "lon"),
            P("lat", "lon"),
            P(None, "mem", "lat", "lon"),
            P(None, "lat", "lon"),
            P("lat", "lon"),
            P("lat", "lon"),
            P("lat", "lon"),
            P(LON_LAT, None),
            P(LON_LAT, None),
            P(LON_LAT, None),
            P(LON_LAT, None),
            P(LON_LAT),
        ),
        out_specs=(P(None, "mem", "lat", "lon"), P(None, "lat", "lon")),
        check_vma=False,
    )
```

time: 84.9 us -> 50.7 us (0.60)
  Pallas kernels: 74.4 us -> 50 us
  local copies, waits for them, and re-layouts: 9.12 us -> 0 us
    pallas_call x3 -> x1, Pallas kernels: 68.8 us -> 44.3 us  [smooth(): pl.pallas_call(functools.partial(smooth_kernel, nlon, nlat), out_shape=(s...]
    unnamed x22 -> x0, local copies, waits for them, and re-layouts: 9.12 us -> none
where the time goes in v3:
time: 50.7 us; the launch traced here: 50.6 us
  Pallas kernels  50 us (99%)
  between operations  0.64 us (1%)
    pallas_call x1, Pallas kernels, smooth(): pl.pallas_call(functools.partial(smooth_kernel, nlon, nlat), out_shape=(s...  44.3 us
    pallas_call x1, Pallas kernels, analysis(): pl.pallas_call(analysis_kernel, grid=(3,), out_shape=(sds((3, own, 16, 25...  5.67 us

profile of v3, /device:TPU:1, one launch (start us, length us, event | category | flops | bytes accessed | tf_op | source)
XLA Modules:
  0.0 50.6 jit_solution(1841862623815297138)
XLA Ops:
  0.6 44.3 %smooth.1 = (bf16[16,128,256]{2,1,0:T(8,128)(2,1)S(1)}, f32[16,8,128]{2,1,0:T(8,128)S(1)}, f32[8,128]{1,0:T(8,128)S(1)}, f32[16,256]{1,0:T(8,128)S(1)}, f32[16,2...) custom-call(bf16[64,16,256]{2,1,0:T(8,128)(2,1)} %anom_in.1, f32[16,256]{1,0:T(8,128)} %mean_in.1, ...), custom_call_target="tpu_custom_call" | custom-call | tf_op jit(solution)/shard_map/smooth/pallas_call | solution.py:482
  45.0 5.7 %analysis.1 = (bf16[3,64,16,256]{3,2,1,0:T(8,128)(2,1)}, f32[3,16,256]{2,1,0:T(8,128)}) custom-call(f32[16,8,128]{2,1,0:T(8,128)S(1)} %get-tuple-element.9.gram, f32[8,128]{1,0:T(8,128)S(1)} %get-tuple-element.10.projection, bf16[16,128,256]{2,1,0:T(8,128)(2,1)S(1)} %get-tuple-element.11.now, bf16[2,16,128,256]{3,2,1,0:T(8,128)(2,1)S(1)} %get-tuple-element.12.lag, ...), custom_call_target="tpu_custom_call" | custom-call | tf_op jit(solution)/shard_map/analysis/pallas_call | solution.py:648

commit v4 on v3

--- a/solution.py
+++ b/solution.py
@@ -85,13 +85,19 @@
     to_south,
     to_north,
     edges,
+    corners,
     field_edges,
+    field_corner,
+    field_south_out,
+    field_north_out,
     from_north,
     from_south,
     beside,
+    beyond,
     field_north,
     field_south,
     field_beside,
+    field_beyond,
     placed,
     midway,
     turned,
@@ -126,7 +132,6 @@
     lon, lat, mem = lax.axis_index("lon"), lax.axis_index("lat"), lax.axis_index("mem")
     twin = spot(lon, lat, 1 - mem)
     members = anom.shape[0]
-    half = members // 2
     base = pl.multiple_of(mem * members, members)
 
     def at(dx, dy, m=mem):
@@ -167,13 +172,22 @@
         load.wait()
     fields[3] = ocean[...].astype(F32)
     wet_out[...] = fields[3]
-    sub = iota((half, 8, 256), 1)
-    top = anom[:, 0:8, :].astype(F32)
-    low = jnp.where(sub < 4, top[:half], pltpu.roll(top[half:], 4, 1))
-    to_south[...] = low.astype(BF)
-    bottom = anom[:, 8:16, :].astype(F32)
-    high = jnp.where(sub < 4, pltpu.roll(bottom[:half], 4, 1), bottom[half:])
-    to_north[...] = high.astype(BF)
+    chunks = members // 16
+
+    def banded(x, above):
+        low, high = x[:, : x.shape[1] // 2], x[:, x.shape[1] // 2 :]
+        if above:
+            low = pltpu.roll(low, 4, 2)
+        else:
+            high = pltpu.roll(high, 4, 2)
+        return jnp.where(iota(low.shape, 2) < 4, low, high)
+
+    top = anom[:, 0:8, :].astype(F32).reshape(chunks, 16, 8, 256)
+    to_south[...] = banded(top, False).astype(BF)
+    bottom = anom[:, 8:16, :].astype(F32).reshape(chunks, 16, 8, 256)
+    to_north[...] = banded(bottom, True).astype(BF)
+    field_south_out[...] = banded(fields[:, 0:8, :].reshape(1, 4, 8, 256), False)[0]
+    field_north_out[...] = banded(fields[:, 8:16, :].reshape(1, 4, 8, 256), True)[0]
     lane16 = iota((16, 128), 1)
 
     def both_edges(x):
@@ -187,9 +201,18 @@
             out = jnp.where(owner, moved, out)
         return out
 
-    field_edges[...] = packed(lambda k: fields[k], 4)
-    for g in range(members // 16):
-        edges[g] = packed(lambda k: anom[16 * g + k].astype(F32), 16).astype(BF)
+    sub8, lane8 = iota((8, 128), 0), iota((8, 128), 1)
+
+    def corner(x):
+        return jnp.where(sub8 < 4, x[0:8], x[8:16])
+
+    packed_fields = packed(lambda k: fields[k], 4)
+    field_edges[...] = packed_fields
+    field_corner[...] = corner(packed_fields)
+    for g in range(chunks):
+        packed_group = packed(lambda k: anom[16 * g + k].astype(F32), 16)
+        edges[g] = packed_group.astype(BF)
+        corners[g] = corner(packed_group).astype(BF)
 
     for load in loads[5:10]:
         load.wait()
@@ -199,8 +222,7 @@
     tile_col = jnp.sum(jnp.where(row_i == col_i, tile_row, 0.0), axis=1, keepdims=True)
     before = (tile_col == tile_row) & (row_i < col_i)
     rank = jnp.sum(jnp.where(before, 1.0, 0.0), axis=0, keepdims=True)
-    wanted = (row_i % nlon) * nlat + row_i // nlon
-    chosen = (wanted.astype(F32) == tile_row) & (rank == mem.astype(F32))
+    chosen = (row_i.astype(F32) == tile_row) & (rank == mem.astype(F32))
     selection = jnp.where(chosen, 1.0, 0.0).astype(BF)
     valid = iota((slots, blocks), 0) < count[...]
     weight = jnp.where(valid, 1.0 / variance[...], 0.0)
@@ -219,46 +241,40 @@
         ],
         axis=0,
     ).astype(BF)
-    spread = lax.dot_general(selection, payload, NT, preferred_element_type=F32).astype(BF)
-    placed[...] = spread.reshape(nlat, nlon, 6 * slots)
+    spread = lax.dot_general(selection, payload, NT, preferred_element_type=F32)
+    placed[...] = spread.reshape(nlon, nlat, 6 * slots).astype(BF)
 
     pl.semaphore_wait(barrier, total)
 
     first = []
-    for d in range(1, nlat):
-        to = lax.rem(lat + d, nlat)
+    for d in range(1, nlon):
+        to = lax.rem(lon + d, nlon)
+        k = d - 1
         first.append(
-            remote(
-                placed.at[to], midway.at[lat], lat_send.at[d - 1], lat_recv.at[d - 1], at(0, d)
-            )
+            remote(placed.at[to], midway.at[lon], lon_send.at[k], lon_recv.at[k], at(d, 0))
         )
     halo = []
-    for i, (dx, dy) in enumerate(SIDES):
-        there = at(-dx, -dy)
-        halo.append(remote(edges, beside.at[i], halo_send.at[i], halo_recv.at[i], there))
-        halo.append(
-            remote(
-                field_edges, field_beside.at[i], halo_send.at[6 + i], halo_recv.at[6 + i], there
-            )
-        )
-    for j, (start, into, dy) in enumerate(((0, field_north, -1), (8, field_south, 1))):
-        part = fields.at[:, pl.ds(start, 8), :]
-        halo.append(remote(part, into, halo_send.at[12 + j], halo_recv.at[12 + j], at(0, dy)))
-    chunks = 4
-    wide_chunk = half // chunks
+    pieces = [(field_south_out, field_north, 0, -1), (field_north_out, field_south, 0, 1)]
+    for i, (dx, dy) in enumerate(SIDES[:2]):
+        pieces.append((edges, beside.at[i], -dx, -dy))
+        pieces.append((field_edges, field_beside.at[i], -dx, -dy))
+    for i, (dx, dy) in enumerate(SIDES[2:]):
+        pieces.append((corners, beyond.at[i], -dx, -dy))
+        pieces.append((field_corner, field_beyond.at[i], -dx, -dy))
+    for i, (src, dst, dx, dy) in enumerate(pieces):
+        halo.append(remote(src, dst, halo_send.at[i], halo_recv.at[i], at(dx, dy)))
     bands = []
     for c in range(chunks):
-        some = pl.ds(c * wide_chunk, wide_chunk)
         for j, (src, dst, dy) in enumerate(
             ((to_south, from_north, -1), (to_north, from_south, 1))
         ):
             k = 2 * c + j
             bands.append(
-                remote(src.at[some], dst.at[some], chunk_send.at[k], chunk_recv.at[k], at(0, dy))
+                remote(src.at[c], dst.at[c], chunk_send.at[k], chunk_recv.at[k], at(0, dy))
             )
-    for copy in first + halo + bands:
+    for copy in halo + bands[:2] + first + bands[2:]:
         copy.start()
-    midway[lat] = placed[lat]
+    midway[lon] = placed[lon]
 
     loads[10].wait()
     loads[11].wait()
@@ -272,41 +288,41 @@
             lag_all[which, r, pl.ds(base, members), :] = row.astype(BF)
         ours = lag_all.at[which, :, pl.ds(base, members), :]
         late.append(remote(ours, ours, pair_send.at[5 + which], pair_recv.at[5 + which], twin))
+        late[-1].start()
 
     for copy in first:
         copy.wait()
-    swap = (row_i // nlat == col_i % nlon) & (row_i % nlat == col_i // nlon)
-    mixed = midway[...].reshape(blocks, 6 * slots)
+    swap = (row_i // nlon == col_i % nlat) & (row_i % nlon == col_i // nlat)
+    mixed = midway[...].astype(F32).reshape(blocks, 6 * slots).astype(BF)
     ordered = jnp.dot(jnp.where(swap, 1.0, 0.0).astype(BF), mixed, preferred_element_type=F32)
-    turned[...] = ordered.reshape(nlon, nlat, 6 * slots).astype(BF)
+    turned[...] = ordered.reshape(nlat, nlon, 6 * slots).astype(BF)
     second = []
-    for d in range(1, nlon):
-        to = lax.rem(lon + d, nlon)
+    for d in range(1, nlat):
+        to = lax.rem(lat + d, nlat)
         copy = remote(
-            turned.at[to], arrived.at[lon], lon_send.at[d - 1], lon_recv.at[d - 1], at(d, 0)
+            turned.at[to], arrived.at[lat], lat_send.at[d - 1], lat_recv.at[d - 1], at(0, d)
         )
         copy.start()
         second.append(copy)
-    arrived[lon] = turned[lon]
-
+    arrived[lat] = turned[lat]
     for copy in halo:
         copy.wait()
     north_ok = lat < nlat - 1
     south_ok = lat > 0
-    sub8, lane8 = iota((8, 128), 0), iota((8, 128), 1)
 
     def sides(east, west, north_east, south_east, north_west, south_west):
         core = jnp.where(lane16 % 8 < 4, east, west)
         is_east = lane8 % 8 < 4
-        up = jnp.where(is_east, north_east[0:8], north_west[0:8])
-        down = jnp.where(is_east, south_east[8:16], south_west[8:16])
+        up = jnp.where(is_east, north_east, north_west)
+        down = jnp.where(is_east, south_east, south_west)
         up = jnp.where(north_ok, up, 0.0)
         down = jnp.where(south_ok, down, 0.0)
         return jnp.concatenate([core, jnp.where(sub8 < 4, up, down)], axis=0)
 
-    for g in range(members // 16):
-        side[g] = sides(*[beside[i, g].astype(F32) for i in range(6)])
-    field_side = sides(*[field_beside[i] for i in range(6)])
+    for g in range(chunks):
+        near = [beside[i, g].astype(F32) for i in range(2)]
+        side[g] = sides(*near, *[beyond[i, g].astype(F32) for i in range(4)])
+    field_side = sides(*[field_beside[i] for i in range(2)], *[field_beyond[i] for i in range(4)])
     lane24 = iota((24, 128), 1)
     keep = (lane24 < 4) | (lane24 >= 124)
     subw = iota((8, 256), 0)
@@ -319,7 +335,12 @@
     for k in range(4):
         turn = pltpu.roll(field_side, 128 - 8 * k, 1) if k else field_side
         turn = jnp.where(keep, turn, 0.0)
-        extended.append(whole(fields[k], field_north[k], field_south[k], turn))
+        up, down = field_north[k % 2], field_south[k % 2]
+        if k < 2:
+            down = pltpu.roll(down, 4, 0)
+        else:
+            up = pltpu.roll(up, 4, 0)
+        extended.append(whole(fields[k], up, down, turn))
     ex_mean, ex_x, ex_y, ex_wet = extended
     coef[0] = ex_wet * jnp.maximum(ex_x, 0.0)
     coef[1] = -ex_wet * jnp.minimum(ex_x, 0.0)
@@ -334,42 +355,48 @@
         north = pltpu.roll(q, q.shape[0] - 1, 0)
         return (coef[4] * q + coef[0] * west) + (coef[1] * east + coef[2] * south) + coef[3] * north
 
-    q = ex_mean
-    for _ in range(SUBSTEPS):
-        q = substep(q)
-    mean_out[...] = q[0:16, 0:256]
-    together = 4
-
-    def some_members(j, carry):
-        where_to, group = [], []
-        for k in range(together):
-            i = j * together + k
-            north, south = from_north[i].astype(F32), from_south[i].astype(F32)
-            for second_half in (False, True):
-                m = i + half if second_half else i
-                up = pltpu.roll(north, 4, 0) if second_half else north
-                down = south if second_half else pltpu.roll(south, 4, 0)
-                turn = lax.rem(128 - 8 * lax.rem(i, 16), 128)
-                turned_side = pltpu.roll(side[m // 16], turn, 1)
-                where_to.append(m)
-                group.append(whole(anom[m].astype(F32), up, down, turned_side))
-        for _ in range(SUBSTEPS):
-            group = [substep(q) for q in group]
-        for m, q in zip(where_to, group):
-            for h in range(2):
-                start = pl.multiple_of((h * members + m) * 16, 16)
-                stage[0, pl.ds(start, 16), :] = q[0:16, 128 * h : 128 * h + 128]
-        return carry
-
-    rounds = wide_chunk // together
+    swaps = []
 
     def advance(c):
         for copy in bands[2 * c : 2 * c + 2]:
             copy.wait()
-        lax.fori_loop(c * rounds, (c + 1) * rounds, some_members, 0)
-
-    for c in range(chunks - 1):
+        where_to, group = [], []
+        for i in range(8):
+            north, south = from_north[c, i].astype(F32), from_south[c, i].astype(F32)
+            for later in (0, 8):
+                m = 16 * c + i + later
+                up = pltpu.roll(north, 4, 0) if later else north
+                down = south if later else pltpu.roll(south, 4, 0)
+                turn = (128 - 8 * (i + later)) % 128
+                turned_side = pltpu.roll(side[c], turn, 1) if turn else side[c]
+                where_to.append(m)
+                group.append(whole(anom[m].astype(F32), up, down, turned_side))
+        if c == 0:
+            group.append(ex_mean)
+        for _ in range(SUBSTEPS):
+            group = [substep(q) for q in group]
+        if c == 0:
+            mean_out[...] = group.pop()[0:16, 0:256]
+        for m, q in zip(where_to, group):
+            for h in range(2):
+                start = (h * members + m) * 16
+                stage[0, start : start + 16, :] = q[0:16, 128 * h : 128 * h + 128]
+        rows = pl.ds(pl.multiple_of(base + 16 * c, 16), 16)
+        for r in range(16):
+            parts_of_row = [
+                stage[0, pl.ds((h * members + 16 * c) * 16 + r, 16, stride=16), :]
+                for h in range(2)
+            ]
+            everyone[r, rows, :] = jnp.concatenate(parts_of_row, axis=1).astype(BF)
+        ours = everyone.at[:, rows, :]
+        swaps.append(remote(ours, ours, pair_send.at[c], pair_recv.at[c], twin))
+        swaps[-1].start()
+
+    advance(0)
+    for c in range(1, chunks - 1):
         advance(c)
+
+    advance(chunks - 1)
 
     for copy in second:
         copy.wait()
@@ -401,16 +428,7 @@
     swap_cells = remote(cell, cell_other, pair_send.at[4], pair_recv.at[4], twin)
     swap_cells.start()
 
-    advance(chunks - 1)
-
-    swaps = []
-    for c in range(4):
-        for r in range(4 * c, 4 * c + 4):
-            row = row_of_all(stage.at[0], r, members).astype(BF)
-            everyone[r, pl.ds(base, members), :] = row
-        ours = everyone.at[pl.ds(4 * c, 4), pl.ds(base, members), :]
-        swaps.append(remote(ours, ours, pair_send.at[c], pair_recv.at[c], twin))
-        swaps[-1].start()
+
     swap_cells.wait()
     sums = cell[...] + cell_other[...]
     weight = sums[0:16]
@@ -420,51 +438,52 @@
         left[r, 0:members] = (x * weight[r : r + 1]).astype(BF)
         left[r, members : members + 16] = jnp.broadcast_to(misfit[r : r + 1], (16, 256)).astype(BF)
     acc = jnp.zeros((members + 16, 2 * members), F32)
-    for c in range(4):
-        swaps[c].wait()
-        for r in range(4 * c, 4 * c + 4):
-            acc = acc + lax.dot_general(left[r], everyone[r], NT, preferred_element_type=F32)
-    for z in range(nlat):
-        parts[z, 0:8] = acc[8 * z : 8 * z + 8]
-        parts[z, 8:9] = acc[members : members + 1]
+    for copy in swaps:
+        copy.wait()
+    for r in range(16):
+        acc = acc + lax.dot_general(left[r], everyone[r], NT, preferred_element_type=F32)
+    own = members // nlon
+    for x in range(nlon):
+        parts[x, 0:own] = acc[own * x : own * x + own]
+        parts[x, own : own + 1] = acc[members : members + 1]
 
     first = []
-    for d in range(1, nlat):
-        to = lax.rem(lat + d, nlat)
+    for d in range(1, nlon):
+        to = lax.rem(lon + d, nlon)
         k = d - 1
-        copy = remote(parts.at[to], got_lat.at[lat], sum_send.at[k], sum_recv.at[k], at(0, d))
+        copy = remote(parts.at[to], got_lon.at[lon], sum_send.at[k], sum_recv.at[k], at(d, 0))
         copy.start()
         first.append(copy)
-    got_lat[lat] = parts[lat]
-    for copy in late:
-        copy.start()
+    got_lon[lon] = parts[lon]
     for copy in first:
-        copy.wait()
-    part = got_lat[0]
-    for z in range(1, nlat):
-        part = part + got_lat[z]
-    mine[...] = part
-
-    second = []
-    for d in range(1, nlon):
-        k = nlat + d - 2
-        copy = remote(mine, got_lon.at[lon], sum_send.at[k], sum_recv.at[k], at(d, 0))
-        copy.start()
-        second.append(copy)
-    got_lon[lon] = part
-    for copy in second:
         copy.wait()
     part = got_lon[0]
     for x in range(1, nlon):
         part = part + got_lon[x]
-    projection[...] = jnp.broadcast_to(part[8:9], projection.shape)
-    slot = mem * nlat + lat
-    gram[slot] = part[0:8]
-    third = []
+    mine[...] = part
+
+    second = []
     for i, (d, m) in enumerate(across):
         copy = remote(
-            gram.at[slot], gram.at[slot], all_send.at[i], all_recv.at[i], at(0, d, other(m))
+            mine, got_lat.at[mem, lat], all_send.at[i], all_recv.at[i], at(0, d, other(m))
         )
+        copy.start()
+        second.append(copy)
+    got_lat[mem, lat] = part
+    for copy in second:
+        copy.wait()
+    totals = []
+    for m in range(2):
+        part = got_lat[m, 0]
+        for z in range(1, nlat):
+            part = part + got_lat[m, z]
+        totals.append(part)
+    projection[...] = jnp.broadcast_to(totals[0][own : own + 1], projection.shape)
+    gram[lon] = jnp.concatenate([t[0:own] for t in totals], axis=0)
+    third = []
+    for d in range(1, nlon):
+        k = nlon + d - 2
+        copy = remote(gram.at[lon], gram.at[lon], sum_send.at[k], sum_recv.at[k], at(d, 0))
         copy.start()
         third.append(copy)
     for copy in third + late:
@@ -483,7 +502,7 @@
         functools.partial(smooth_kernel, nlon, nlat),
         out_shape=(
             sds((16, pair, 256), BF),
-            sds((2 * nlat, 8, pair), F32),
+            sds((nlon, 2 * members // nlon, pair), F32),
             sds((8, pair), F32),
             sds((16, 256), F32),
             sds((16, 256), F32),
@@ -502,20 +521,26 @@
             pltpu.VMEM((1, blocks), jnp.int32),
             pltpu.VMEM((1, blocks), jnp.int32),
             pltpu.VMEM((2, members, 16, 256), BF),
-            pltpu.VMEM((members // 2, 8, 256), BF),
-            pltpu.VMEM((members // 2, 8, 256), BF),
+            pltpu.VMEM((members // 16, 8, 8, 256), BF),
+            pltpu.VMEM((members // 16, 8, 8, 256), BF),
             pltpu.VMEM((members // 16, 16, 128), BF),
+            pltpu.VMEM((members // 16, 8, 128), BF),
             pltpu.VMEM((16, 128), F32),
-            pltpu.VMEM((members // 2, 8, 256), BF),
-            pltpu.VMEM((members // 2, 8, 256), BF),
-            pltpu.VMEM((6, members // 16, 16, 128), BF),
-            pltpu.VMEM((4, 8, 256), F32),
-            pltpu.VMEM((4, 8, 256), F32),
-            pltpu.VMEM((6, 16, 128), F32),
+            pltpu.VMEM((8, 128), F32),
+            pltpu.VMEM((2, 8, 256), F32),
+            pltpu.VMEM((2, 8, 256), F32),
+            pltpu.VMEM((members // 16, 8, 8, 256), BF),
+            pltpu.VMEM((members // 16, 8, 8, 256), BF),
+            pltpu.VMEM((2, members // 16, 16, 128), BF),
+            pltpu.VMEM((4, members // 16, 8, 128), BF),
+            pltpu.VMEM((2, 8, 256), F32),
+            pltpu.VMEM((2, 8, 256), F32),
+            pltpu.VMEM((2, 16, 128), F32),
+            pltpu.VMEM((4, 8, 128), F32),
+            pltpu.VMEM((nlon, nlat, lanes), BF),
+            pltpu.VMEM((nlon, nlat, lanes), BF),
             pltpu.VMEM((nlat, nlon, lanes), BF),
             pltpu.VMEM((nlat, nlon, lanes), BF),
-            pltpu.VMEM((nlon, nlat, lanes), BF),
-            pltpu.VMEM((nlon, nlat, lanes), BF),
             pltpu.VMEM((2, members * 32, 128), F32),
             pltpu.VMEM((5, 24, 384), F32),
             pltpu.VMEM((members // 16, 24, 128), F32),
@@ -523,10 +548,10 @@
             pltpu.VMEM((32, 256), F32),
             pltpu.VMEM((32, 256), F32),
             pltpu.VMEM((16, members + 16, 256), BF),
-            pltpu.VMEM((nlat, 9, pair), F32),
-            pltpu.VMEM((nlat, 9, pair), F32),
-            pltpu.VMEM((9, pair), F32),
-            pltpu.VMEM((nlon, 9, pair), F32),
+            pltpu.VMEM((nlon, members // nlon + 1, pair), F32),
+            pltpu.VMEM((2, nlat, members // nlon + 1, pair), F32),
+            pltpu.VMEM((members // nlon + 1, pair), F32),
+            pltpu.VMEM((nlon, members // nlon + 1, pair), F32),
             dma((12,)),
             dma((14,)),
             dma((14,)),
@@ -538,8 +563,8 @@
             dma((nlon - 1,)),
             dma((7,)),
             dma((7,)),
-            dma((nlon + nlat - 2,)),
-            dma((nlon + nlat - 2,)),
+            dma((2 * nlon - 2,)),
+            dma((2 * nlon - 2,)),
             dma((2 * nlat - 1,)),
             dma((2 * nlat - 1,)),
         ],
@@ -603,7 +628,12 @@
     @pl.when(step == 0)
     def _():
         n = members
-        root, weights = inverse_root(gram[...].reshape(n, n), projection[0:1])
+        few = gram.shape[1] // 2
+        for x in range(gram.shape[0]):
+            for m in range(2):
+                start = m * own + few * x
+                transform[start : start + few] = gram[x, few * m : few * m + few]
+        root, weights = inverse_root(transform[...], projection[0:1])
         transform[...] = jnp.sqrt(n - 1.0) * root
         left[0:own] = transform[pl.ds(base, own), :].astype(BF)
         left[own : own + 16] = jnp.broadcast_to(weights, (16, n)).astype(BF)

time: 50.7 us -> 47.6 us (0.939)
  Pallas kernels: 50 us -> 46.8 us
    pallas_call x1, Pallas kernels: 44.3 us -> 41.1 us  [smooth(): pl.pallas_call(functools.partial(smooth_kernel, nlon, nlat), out_shape=(s...]
where the time goes in v4:
time: 47.6 us; the launch traced here: 47.5 us
  Pallas kernels  46.8 us (98%)
  between operations  0.64 us (1%)
    pallas_call x1, Pallas kernels, smooth(): pl.pallas_call(functools.partial(smooth_kernel, nlon, nlat), out_shape=(s...  41.1 us
    pallas_call x1, Pallas kernels, analysis(): pl.pallas_call(analysis_kernel, grid=(3,), out_shape=(sds((3, own, 16, 25...  5.68 us

profile of v4, /device:TPU:1, one launch (start us, length us, event | category | flops | bytes accessed | tf_op | source)
XLA Modules:
  0.0 47.5 jit_solution(12022368707392390040)
XLA Ops:
  0.6 41.1 %smooth.1 = (bf16[16,128,256]{2,1,0:T(8,128)(2,1)S(1)}, f32[16,8,128]{2,1,0:T(8,128)S(1)}, f32[8,128]{1,0:T(8,128)S(1)}, f32[16,256]{1,0:T(8,128)S(1)}, f32[16,2...) custom-call(bf16[64,16,256]{2,1,0:T(8,128)(2,1)} %anom_in.1, f32[16,256]{1,0:T(8,128)} %mean_in.1, ...), custom_call_target="tpu_custom_call" | custom-call | tf_op jit(solution)/shard_map/smooth/pallas_call | solution.py:501
  41.8 5.7 %analysis.1 = (bf16[3,64,16,256]{3,2,1,0:T(8,128)(2,1)}, f32[3,16,256]{2,1,0:T(8,128)}) custom-call(f32[16,8,128]{2,1,0:T(8,128)S(1)} %get-tuple-element.9.gram, f32[8,128]{1,0:T(8,128)S(1)} %get-tuple-element.10.projection, bf16[16,128,256]{2,1,0:T(8,128)(2,1)S(1)} %get-tuple-element.11.now, bf16[2,16,128,256]{3,2,1,0:T(8,128)(2,1)S(1)} %get-tuple-element.12.lag, ...), custom_call_target="tpu_custom_call" | custom-call | tf_op jit(solution)/shard_map/analysis/pallas_call | solution.py:678

commit v5 on v4

--- a/solution.py
+++ b/solution.py
@@ -156,7 +156,7 @@
             )
         )
     ]
-    for load in loads:
+    for load in loads[:5]:
         load.start()
     across = [(d, m) for m in (0, 1) for d in range(nlat) if d or m]
 
@@ -167,6 +167,8 @@
     peers += [at(d, 0) for d in range(1, nlon)]
     peers += [at(dx, dy) for dx, dy in SIDES if dy != 0]
     barrier, total = greet(peers)
+    for load in loads[5:]:
+        load.start()
 
     for load in loads[:5]:
         load.wait()
@@ -214,6 +216,36 @@
         edges[g] = packed_group.astype(BF)
         corners[g] = corner(packed_group).astype(BF)
 
+    pl.semaphore_wait(barrier, total)
+
+    first = []
+    for d in range(1, nlon):
+        to = lax.rem(lon + d, nlon)
+        k = d - 1
+        first.append(
+            remote(placed.at[to], midway.at[lon], lon_send.at[k], lon_recv.at[k], at(d, 0))
+        )
+    halo = []
+    pieces = [(field_south_out, field_north, 0, -1), (field_north_out, field_south, 0, 1)]
+    for i, (dx, dy) in enumerate(SIDES[:2]):
+        pieces.append((edges, beside.at[i], -dx, -dy))
+        pieces.append((field_edges, field_beside.at[i], -dx, -dy))
+    for i, (dx, dy) in enumerate(SIDES[2:]):
+        pieces.append((corners, beyond.at[i], -dx, -dy))
+        pieces.append((field_corner, field_beyond.at[i], -dx, -dy))
+    for i, (src, dst, dx, dy) in enumerate(pieces):
+        halo.append(remote(src, dst, halo_send.at[i], halo_recv.at[i], at(dx, dy)))
+    bands = []
+    for c in range(chunks):
+        for j, (src, dst, dy) in enumerate(
+            ((to_south, from_north, -1), (to_north, from_south, 1))
+        ):
+            k = 2 * c + j
+            bands.append(
+                remote(src.at[c], dst.at[c], chunk_send.at[k], chunk_recv.at[k], at(0, dy))
+            )
+    for copy in halo + bands:
+        copy.start()
     for load in loads[5:10]:
         load.wait()
     slots, blocks = values.shape
@@ -244,35 +276,7 @@
     spread = lax.dot_general(selection, payload, NT, preferred_element_type=F32)
     placed[...] = spread.reshape(nlon, nlat, 6 * slots).astype(BF)
 
-    pl.semaphore_wait(barrier, total)
-
-    first = []
-    for d in range(1, nlon):
-        to = lax.rem(lon + d, nlon)
-        k = d - 1
-        first.append(
-            remote(placed.at[to], midway.at[lon], lon_send.at[k], lon_recv.at[k], at(d, 0))
-        )
-    halo = []
-    pieces = [(field_south_out, field_north, 0, -1), (field_north_out, field_south, 0, 1)]
-    for i, (dx, dy) in enumerate(SIDES[:2]):
-        pieces.append((edges, beside.at[i], -dx, -dy))
-        pieces.append((field_edges, field_beside.at[i], -dx, -dy))
-    for i, (dx, dy) in enumerate(SIDES[2:]):
-        pieces.append((corners, beyond.at[i], -dx, -dy))
-        pieces.append((field_corner, field_beyond.at[i], -dx, -dy))
-    for i, (src, dst, dx, dy) in enumerate(pieces):
-        halo.append(remote(src, dst, halo_send.at[i], halo_recv.at[i], at(dx, dy)))
-    bands = []
-    for c in range(chunks):
-        for j, (src, dst, dy) in enumerate(
-            ((to_south, from_north, -1), (to_north, from_south, 1))
-        ):
-            k = 2 * c + j
-            bands.append(
-                remote(src.at[c], dst.at[c], chunk_send.at[k], chunk_recv.at[k], at(0, dy))
-            )
-    for copy in halo + bands[:2] + first + bands[2:]:
+    for copy in first:
         copy.start()
     midway[lon] = placed[lon]
 
@@ -348,12 +352,27 @@
     coef[3] = -ex_wet * jnp.minimum(ex_y, 0.0)
     coef[4] = 1.0 - ((coef[0] + coef[1]) + (coef[2] + coef[3]))
 
-    def substep(q):
-        west = pltpu.roll(q, 1, 1)
-        east = pltpu.roll(q, q.shape[1] - 1, 1)
-        south = pltpu.roll(q, 1, 0)
-        north = pltpu.roll(q, q.shape[0] - 1, 0)
-        return (coef[4] * q + coef[0] * west) + (coef[1] * east + coef[2] * south) + coef[3] * north
+    def substep(group):
+        tiles = [
+            [[q[8 * r : 8 * r + 8, 128 * c : 128 * c + 128] for c in range(3)] for r in range(3)]
+            for q in group
+        ]
+        new = [[[None] * 3 for _ in range(3)] for _ in group]
+        for r in range(3):
+            for c in range(3):
+                a, b, d, e, keep_own = [
+                    coef[k, 8 * r : 8 * r + 8, 128 * c : 128 * c + 128] for k in range(5)
+                ]
+                for t, out in zip(tiles, new):
+                    q = t[r][c]
+                    west = pltpu.roll(jnp.where(lane8 == 127, t[r][c - 1], q), 1, 1)
+                    east = pltpu.roll(jnp.where(lane8 == 0, t[r][(c + 1) % 3], q), 127, 1)
+                    south = pltpu.roll(jnp.where(sub8 == 7, t[r - 1][c], q), 1, 0)
+                    north = pltpu.roll(jnp.where(sub8 == 0, t[(r + 1) % 3][c], q), 7, 0)
+                    out[r][c] = (keep_own * q + a * west) + (b * east + d * south) + e * north
+        return [
+            jnp.concatenate([jnp.concatenate(row, axis=1) for row in out], axis=0) for out in new
+        ]
 
     swaps = []
 
@@ -374,7 +393,7 @@
         if c == 0:
             group.append(ex_mean)
         for _ in range(SUBSTEPS):
-            group = [substep(q) for q in group]
+            group = sum([substep(group[k : k + 4]) for k in range(0, len(group), 4)], [])
         if c == 0:
             mean_out[...] = group.pop()[0:16, 0:256]
         for m, q in zip(where_to, group):
@@ -422,7 +441,7 @@
         rhs = jnp.where(col_id == two(5), 1.0, 0.0)
         return acc + lax.dot_general(lhs.astype(BF), rhs.astype(BF), NT, preferred_element_type=F32)
 
-    acc = lax.fori_loop(0, pairs // 2, histogram, jnp.zeros((64, 256), F32), unroll=8)
+    acc = lax.fori_loop(0, pairs // 2, histogram, jnp.zeros((64, 256), F32), unroll=16)
     cell[0:16] = acc[0:16] + acc[16:32]
     cell[16:32] = acc[32:48] + acc[48:64]
     swap_cells = remote(cell, cell_other, pair_send.at[4], pair_recv.at[4], twin)

time: 47.6 us -> 47.2 us (level)
  no operation moved by 1% of the time
where the time goes in v5:
time: 47.2 us; the launch traced here: 47.1 us
  Pallas kernels  46.5 us (99%)
  between operations  0.64 us (1%)
    pallas_call x1, Pallas kernels, smooth(): pl.pallas_call(functools.partial(smooth_kernel, nlon, nlat), out_shape=(s...  40.8 us
    pallas_call x1, Pallas kernels, analysis(): pl.pallas_call(analysis_kernel, grid=(3,), out_shape=(sds((3, own, 16, 25...  5.69 us

profile of v5, /device:TPU:1, one launch (start us, length us, event | category | flops | bytes accessed | tf_op | source)
XLA Modules:
  0.0 47.1 jit_solution(6177433482182102181)
XLA Ops:
  0.6 40.8 %smooth.1 = (bf16[16,128,256]{2,1,0:T(8,128)(2,1)S(1)}, f32[16,8,128]{2,1,0:T(8,128)S(1)}, f32[8,128]{1,0:T(8,128)S(1)}, f32[16,256]{1,0:T(8,128)S(1)}, f32[16,2...) custom-call(bf16[64,16,256]{2,1,0:T(8,128)(2,1)} %anom_in.1, f32[16,256]{1,0:T(8,128)} %mean_in.1, ...), custom_call_target="tpu_custom_call" | custom-call | tf_op jit(solution)/shard_map/smooth/pallas_call | solution.py:520
  41.4 5.7 %analysis.1 = (bf16[3,64,16,256]{3,2,1,0:T(8,128)(2,1)}, f32[3,16,256]{2,1,0:T(8,128)}) custom-call(f32[16,8,128]{2,1,0:T(8,128)S(1)} %get-tuple-element.9.gram, f32[8,128]{1,0:T(8,128)S(1)} %get-tuple-element.10.projection, bf16[16,128,256]{2,1,0:T(8,128)(2,1)S(1)} %get-tuple-element.11.now, bf16[2,16,128,256]{3,2,1,0:T(8,128)(2,1)S(1)} %get-tuple-element.12.lag, ...), custom_call_target="tpu_custom_call" | custom-call | tf_op jit(solution)/shard_map/analysis/pallas_call | solution.py:697
